TPU v7x, 256 devices: a whole 4x4x8 slice. The times are simulated.
256 devices in a mesh: gz: 64 (over x, z, y_hi), gx: 4 (over y_lo, core).
Axes of the slice: x: 4, y: 4 (y_hi: 2, y_lo: 2; y = y_hi * 2 + y_lo), z: 8, core: 2. Of those that a mesh axis runs over, the one named last changes fastest.
Arguments:
- velocity: float32 [3, 1024, 64, 128], P(None, 'gz', 'gx'), may hold values from -6 to 6
- pressure: float32 [1024, 64, 128], P('gz', 'gx'), may hold values from -6 to 6
- void_fraction: float32 [1024, 64, 128], P('gz', 'gx'), may hold values from 0.4 to 0.95
- history: float32 [2, 3, 1024, 64, 128], P(None, None, 'gz', 'gx'), may hold values from -6 to 6
- remap_list: int32 [64, 4, 8], replicated, may hold values from 0 to 23, as said below
- parcel_records: float32 [16, 1048576], P(None, ('gz', 'gx')), may hold values from -1 to 1
- parcel_owner: int32 [1048576, 1], P(('gz', 'gx')), may hold values from 0 to 63; in each aligned block of 4096 rows (0 to 4095, 4096 to 8191, ...) at most 128 rows name the same one
- parcel_cells: int32 [1048576], P(('gz', 'gx')), may hold values from 0 to 32767
Outputs:
- new_velocity: float32 [3, 1024, 64, 128], P(None, 'gz', 'gx')
- new_pressure: float32 [1024, 64, 128], P('gz', 'gx')
- new_history: float32 [2, 3, 1024, 64, 128], P(None, None, 'gz', 'gx')
Inputs may be any that keep to these rules, and one draw needn't show every extreme that they name: `remap_list`: entries are (o + 1) * 8 + s with o in -1, 0, 1; the new bricks are a permutation of the old ones, and in every draw exactly 1 new bricks of each device come from each of its two neighbours along gz (o = -1 and o = +1). `parcel_owner`: of the 4096 parcels of one device, at most 128 have the same owner.
All inputs are finite; a program needn't handle non-finite values.
Results may differ from a plain program's by a relative error of at most 0.00012.
Values sent between devices are 32-bit elements; how exact they have to be, the bound alone decides.
No kernel may reach another device: no remote copies, remote signals or barrier semaphores. Data moves between devices by JAX's collectives and lax.ppermute only.
A program may use at most 128 MiB of HBM per device.

v0:
```python
import jax
import jax.numpy as jnp
from jax import lax
from jax.experimental import pallas as pl
from jax.experimental.pallas import tpu as pltpu
from jax.sharding import PartitionSpec as P

SWEEPS = 6
TIME_STEP = 0.25
VISCOSITY = 0.5
DRAG_SCALE = 0.5
RELAXATION = 0.8
WEIGHT_NEW = 23.0 / 12.0
WEIGHT_LAST = 16.0 / 12.0
WEIGHT_OLDER = 5.0 / 12.0

BRICK = 16
BRICKS = 8
EDGE = 16
LANES = 128
ROWS = 8
HALO = SWEEPS + 1
WIDE = HALO + EDGE + HALO
REACH = SWEEPS
SPAN = REACH + EDGE + REACH
FIELDS = 11
OWNERS = 64
CAP = 128
PARCELS = 4096
BLOCK = 256
VMEM_LIMIT = 48 * 1024 * 1024

F32 = jnp.float32
BF16 = jnp.bfloat16


def call(kernel, outs, args, smem=(), scratch=()):
    specs = [
        pl.BlockSpec(memory_space=pltpu.SMEM if number in smem else pltpu.VMEM)
        for number in range(len(args))
    ]
    return pl.pallas_call(
        kernel,
        out_shape=[jax.ShapeDtypeStruct(shape, F32) for shape in outs],
        in_specs=specs,
        out_specs=[pl.BlockSpec(memory_space=pltpu.VMEM) for _ in outs],
        scratch_shapes=list(scratch),
        compiler_params=pltpu.CompilerParams(vmem_limit_bytes=VMEM_LIMIT),
    )(*args)


def lane_of():
    return lax.broadcasted_iota(jnp.int32, (ROWS, LANES), 1)


def take(block, index):
    return jnp.take_along_axis(block, index, axis=1, mode="promise_in_bounds")


def field_block(refs, field, tile):
    velocity, history, pressure, void = refs
    layer, half = tile // 2, tile % 2
    rows = slice(half * ROWS, (half + 1) * ROWS)
    if field < 3:
        return velocity[field, layer, rows, :]
    if field < 9:
        return history[(field - 3) // 3, field % 3, layer, rows, :]
    return (pressure if field == 9 else void)[layer, rows, :]


def pack_kernel(codes, velocity, history, pressure, void, to_upper, to_lower):
    cycle = lax.axis_index("gz")
    line = lax.axis_index("gx")
    size = lax.axis_size("gz")
    upper = lax.rem(cycle + 1, size)
    lower = lax.rem(cycle + size - 1, size)
    slot_up = jnp.int32(0)
    slot_down = jnp.int32(0)
    for brick in range(BRICKS):
        code = codes[line * BRICKS + brick, upper]
        slot_up = slot_up + jnp.where(code < BRICKS, code, 0)
        code = codes[line * BRICKS + brick, lower]
        slot_down = slot_down + jnp.where(code >= 2 * BRICKS, code - 2 * BRICKS, 0)
    lane = lane_of()
    group = lane // BRICK
    index_up = slot_up * BRICK + lane % BRICK
    index_down = slot_down * BRICK + lane % BRICK
    refs = (velocity, history, pressure, void)
    for field in range(FIELDS):
        for part in range(4):
            up = jnp.zeros((ROWS, LANES), F32)
            down = jnp.zeros((ROWS, LANES), F32)
            for place in range(8):
                block = field_block(refs, field, part * 8 + place)
                up = jnp.where(group == place, take(block, index_up), up)
                down = jnp.where(group == place, take(block, index_down), down)
            row = (field * 4 + part) * ROWS
            to_upper[row : row + ROWS, :] = up
            to_lower[row : row + ROWS, :] = down


def remap_kernel(
    codes, velocity, history, pressure, void, lower, upper,
    flow_out, latest_out, base_out, press_out, void_out, to_upper, to_lower,
):
    cycle = lax.axis_index("gz")
    line = lax.axis_index("gx")
    lane = lane_of()
    group = lane // BRICK
    code_of = jnp.zeros((ROWS, LANES), jnp.int32)
    for brick in range(BRICKS):
        code_of = jnp.where(group == brick, codes[line * BRICKS + brick, cycle], code_of)
    from_lower = code_of < BRICKS
    from_upper = code_of >= 2 * BRICKS
    index_own = (code_of % BRICKS) * BRICK + lane % BRICK
    refs = (velocity, history, pressure, void)
    for tile in range(32):
        part, place = tile // 8, tile % 8
        index_in = place * BRICK + lane % BRICK
        layer, half = tile // 2, tile % 2
        rows = slice(half * ROWS, (half + 1) * ROWS)
        moved = []
        for field in range(FIELDS):
            row = (field * 4 + part) * ROWS
            own = take(field_block(refs, field, tile), index_own)
            low = take(lower[row : row + ROWS, :], index_in)
            high = take(upper[row : row + ROWS, :], index_in)
            moved.append(jnp.where(from_lower, low, jnp.where(from_upper, high, own)))
        press, void_new = moved[9], moved[10]
        press_out[layer, rows, :] = press
        void_out[layer, rows, :] = void_new
        for axis_no in range(3):
            flow, latest, older = moved[axis_no], moved[3 + axis_no], moved[6 + axis_no]
            flow_out[axis_no, layer, rows, :] = flow
            latest_out[axis_no, layer, rows, :] = latest
            base_out[axis_no, layer, rows, :] = flow + TIME_STEP * (
                WEIGHT_OLDER * older - WEIGHT_LAST * latest
            )
            if layer == 0:
                to_lower[2 * HALO + axis_no, rows, :] = void_new * flow
            if layer == EDGE - 1:
                to_upper[2 * HALO + axis_no, rows, :] = void_new * flow
        if layer < HALO:
            to_lower[layer, rows, :] = void_new
            to_lower[HALO + layer, rows, :] = press
        if layer >= EDGE - HALO:
            to_upper[layer - EDGE + HALO, rows, :] = void_new
            to_upper[2 * HALO + layer - EDGE, rows, :] = press


def pack_rows_kernel(flow, press, void, lower, upper, to_right, to_left):
    for send, rows, edge in ((to_right, slice(8, 16), EDGE - 1), (to_left, slice(0, 8), 0)):
        for number, own in ((0, void), (1, press)):
            start = number * WIDE * ROWS
            for layer in range(HALO):
                row = start + layer * ROWS
                send[row : row + ROWS, :] = lower[number * HALO + layer, rows, :]
                row = start + (HALO + EDGE + layer) * ROWS
                send[row : row + ROWS, :] = upper[number * HALO + layer, rows, :]
            for layer in range(EDGE):
                row = start + (HALO + layer) * ROWS
                send[row : row + ROWS, :] = own[layer, rows, :]
        for axis_no in range(3):
            row = 2 * WIDE * ROWS + axis_no * EDGE
            send[row : row + EDGE, :] = void[:, edge, :] * flow[axis_no, :, edge, :]


def split_two(value):
    high = value.astype(BF16)
    return high, (value - high.astype(F32)).astype(BF16)


NT = (((1,), (1,)), ((), ()))


def dispatch_kernel(records, owners, cells, out, shown, total):
    blocks = PARCELS // BLOCK
    owner_iota = lax.broadcasted_iota(jnp.int32, (OWNERS, BLOCK), 0)
    before = (
        lax.broadcasted_iota(jnp.int32, (BLOCK, BLOCK), 0)
        < lax.broadcasted_iota(jnp.int32, (BLOCK, BLOCK), 1)
    ).astype(F32).astype(BF16)

    def row_of(ref, block):
        return jnp.concatenate([ref[2 * block : 2 * block + 1, :], ref[2 * block + 1 : 2 * block + 2, :]], axis=1)

    for block in range(blocks):
        hit = (row_of(owners, block) == owner_iota).astype(F32)
        shown[block * OWNERS : (block + 1) * OWNERS, :] = hit.astype(BF16)
    earlier = lax.dot_general(
        shown[...], before, (((1,), (0,)), ((), ())), preferred_element_type=F32
    )
    base = jnp.zeros((OWNERS, 1), F32)
    row_iota = lax.broadcasted_iota(jnp.int32, (4, BLOCK), 0)
    key_iota = lax.broadcasted_iota(jnp.int32, (2 * CAP, BLOCK), 0)
    total[...] = jnp.zeros_like(total)
    for block in range(blocks):
        rows = slice(block * OWNERS, (block + 1) * OWNERS)
        hit = shown[rows, :].astype(F32)
        seen = earlier[block * OWNERS : (block + 1) * OWNERS, :]
        rank = jnp.sum(hit * (seen + base), axis=0, keepdims=True).astype(jnp.int32)
        base = base + seen[:, BLOCK - 1 : BLOCK] + hit[:, BLOCK - 1 : BLOCK]
        owner = row_of(owners, block)
        cell = row_of(cells, block)
        key = (owner // 32) * CAP + rank
        placed = (key == key_iota).astype(F32).astype(BF16)
        lanes = slice(block * BLOCK, (block + 1) * BLOCK)
        terms = jnp.zeros((4, BLOCK), F32)
        for size_class in range(4):
            state = records[4 * size_class : 4 * size_class + 4, lanes]
            coefficient = DRAG_SCALE * jnp.exp(state[3:4, :])
            terms = terms + coefficient * jnp.where(row_iota == 3, 1.0, state)
        depth, across, along = cell // 2048, (cell // LANES) % EDGE, cell % LANES
        major = (depth * 8 + across % 8).astype(F32)
        minor = ((across // 8) * LANES + along).astype(F32)
        blank2 = jnp.zeros((2, BLOCK), F32)
        blank4 = jnp.zeros((4, BLOCK), F32)
        coarse = terms.astype(BF16).astype(F32)
        values = jnp.concatenate(
            [coarse, major, minor, blank2, terms - coarse, blank4], axis=0
        ).astype(BF16)
        group = jnp.broadcast_to(owner % 32, (16, BLOCK)).astype(F32).astype(BF16)
        spread = jnp.concatenate(
            [jnp.where(group == jnp.asarray(number, BF16), values, jnp.zeros_like(values)) for number in range(32)],
            axis=0,
        )
        total[...] += lax.dot_general(spread, placed, NT, preferred_element_type=F32)
    for owner in range(OWNERS):
        row = (owner % 32) * 16
        lanes = slice((owner // 32) * CAP, (owner // 32 + 1) * CAP)
        out[owner, :, :] = total[row : row + 8, lanes] + total[row + 8 : row + 16, lanes]


def deposit_kernel(arrived, out, total):
    step = 4
    width = step * CAP
    iota_major = lax.broadcasted_iota(jnp.int32, (128, width), 0).astype(F32).astype(BF16)
    iota_minor = lax.broadcasted_iota(jnp.int32, (256, width), 0).astype(F32).astype(BF16)
    total[...] = jnp.zeros_like(total)
    zero = jnp.zeros((128, width), BF16)

    def body(number, carry):
        def row_of(channel):
            return jnp.concatenate(
                [arrived[number * step + source, channel : channel + 1, :] for source in range(step)], axis=1
            )

        major = jnp.broadcast_to(row_of(4), (128, width)).astype(BF16)
        minor = jnp.broadcast_to(row_of(5), (256, width)).astype(BF16)
        placed = jnp.where(minor == iota_minor, jnp.ones((256, width), BF16), jnp.zeros((256, width), BF16))
        here = major == iota_major
        for channel in range(4):
            value = row_of(channel)
            coarse = value.astype(BF16).astype(F32)
            for part, piece in ((0, coarse), (1, value - coarse)):
                spread = jnp.where(here, jnp.broadcast_to(piece, (128, width)).astype(BF16), zero)
                row = (channel * 2 + part) * 128
                total[row : row + 128, :] += lax.dot_general(spread, placed, NT, preferred_element_type=F32)
        return carry

    lax.fori_loop(0, OWNERS // step, body, 0)
    for channel in range(4):
        row = channel * 256
        for half in range(2):
            lanes = slice(half * LANES, (half + 1) * LANES)
            summed = total[row : row + 128, lanes] + total[row + 128 : row + 256, lanes]
            out[channel, :, half * ROWS : (half + 1) * ROWS, :] = summed.reshape(EDGE, ROWS, LANES)


def lane_up(value):
    lane = lax.broadcasted_iota(jnp.int32, value.shape, 1)
    return jnp.where(lane == LANES - 1, 0.0, pltpu.roll(value, LANES - 1, 1))


def lane_down(value):
    lane = lax.broadcasted_iota(jnp.int32, value.shape, 1)
    return jnp.where(lane == 0, 0.0, pltpu.roll(value, 1, 1))


def row_up(value, after):
    count = value.shape[0]
    row = lax.broadcasted_iota(jnp.int32, value.shape, 0)
    return jnp.where(row == count - 1, after, pltpu.roll(value, count - 1, 0))


def row_down(value, before):
    row = lax.broadcasted_iota(jnp.int32, value.shape, 0)
    return jnp.where(row == 0, before, pltpu.roll(value, 1, 0))


M_LOW = 2 * HALO
M_ROWS = 2 * WIDE * ROWS


def rate_kernel(
    flow, latest, base, void, lower, upper, left, right, deposit,
    history_out, trial_out, div_out, to_upper, to_lower, edge_out, scaled,
):
    def void_layer(layer):
        if layer < 0:
            return lower[HALO + layer, :, :]
        if layer >= EDGE:
            return upper[layer - EDGE, :, :]
        return void[layer, :, :]

    def moment_layer(axis_no, layer):
        if layer < 0:
            return lower[M_LOW + axis_no, :, :]
        if layer >= EDGE:
            return upper[M_LOW + axis_no, :, :]
        return void[layer, :, :] * flow[axis_no, layer, :, :]

    for layer in range(EDGE):
        own = void[layer, :, :]
        row = (HALO + layer) * ROWS
        void_left = left[row + ROWS - 1 : row + ROWS, :]
        void_right = right[row : row + 1, :]
        near = (
            void_layer(layer + 1), void_layer(layer - 1),
            row_up(own, void_right), row_down(own, void_left),
            lane_up(own), lane_down(own),
        )
        around = near[0] + near[1] + near[2] + near[3] + near[4] + near[5]
        inverse = 1.0 / own
        drag = deposit[3, layer, :, :]
        slope = None
        for axis_no in range(3):
            mine = flow[axis_no, layer, :, :]
            moment = own * mine
            row = M_ROWS + axis_no * EDGE + layer
            summed = (
                moment_layer(axis_no, layer + 1) + moment_layer(axis_no, layer - 1)
                + row_up(moment, right[row : row + 1, :]) + row_down(moment, left[row : row + 1, :])
                + lane_up(moment) + lane_down(moment)
            )
            rate = VISCOSITY * (summed - mine * around) + (
                deposit[axis_no, layer, :, :] - drag * mine
            ) * inverse
            history_out[0, axis_no, layer, :, :] = rate
            history_out[1, axis_no, layer, :, :] = latest[axis_no, layer, :, :]
            trial = base[axis_no, layer, :, :] + (TIME_STEP * WEIGHT_NEW) * rate
            trial_out[axis_no, layer, :, :] = trial
            part = trial * (near[2 * axis_no] - near[2 * axis_no + 1])
            slope = part if axis_no == 0 else slope + part
            weighted = own * trial
            if axis_no == 0:
                scaled[layer, :, :] = weighted
            if axis_no == 1:
                slope = slope + row_up(weighted, 0.0) - row_down(weighted, 0.0)
                edge_out[0, layer : layer + 1, :] = weighted[0:1, :]
                edge_out[1, layer : layer + 1, :] = weighted[EDGE - 1 : EDGE, :]
            if axis_no == 2:
                slope = slope + lane_up(weighted) - lane_down(weighted)
        div_out[layer, :, :] = slope
    for layer in range(EDGE):
        total = div_out[layer, :, :]
        if layer < EDGE - 1:
            total = total + scaled[layer + 1, :, :]
        if layer > 0:
            total = total - scaled[layer - 1, :, :]
        div_out[layer, :, :] = total
        if layer < REACH:
            to_lower[layer, :, :] = total
        if layer >= EDGE - REACH:
            to_upper[layer - EDGE + REACH, :, :] = total
    for send, layer, start in ((to_lower, 0, 0), (to_upper, EDGE - 1, EDGE - REACH)):
        send[REACH, :, :] = scaled[layer, :, :]
        for side in range(2):
            send[REACH + 1, side * 8 : side * 8 + REACH, :] = edge_out[side, start : start + REACH, :]
            send[REACH + 1, side * 8 + REACH : side * 8 + 8, :] = jnp.zeros((8 - REACH, LANES), F32)


def pack_div_kernel(div, sent_lower, sent_upper, edge, lower, upper, wide_out, to_right, to_left):
    for layer in range(SPAN):
        if layer < REACH:
            value = lower[layer, :, :]
            if layer == REACH - 1:
                value = value + sent_lower[REACH, :, :]
        elif layer < REACH + EDGE:
            value = div[layer - REACH, :, :]
            if layer == REACH:
                value = value - lower[REACH, :, :]
            if layer == REACH + EDGE - 1:
                value = value + upper[REACH, :, :]
        else:
            value = upper[layer - REACH - EDGE, :, :]
            if layer == REACH + EDGE:
                value = value - sent_upper[REACH, :, :]
        wide_out[layer, :, :] = value
        row = layer * ROWS
        to_right[row : row + ROWS, :] = value[8:16, :]
        to_left[row : row + ROWS, :] = value[0:8, :]
    start = SPAN * ROWS
    for send, side in ((to_left, 0), (to_right, 1)):
        for layer in range(REACH):
            row = start + layer
            send[row : row + 1, :] = lower[REACH + 1, side * 8 + layer : side * 8 + layer + 1, :]
            row = start + REACH + EDGE + layer
            send[row : row + 1, :] = upper[REACH + 1, side * 8 + layer : side * 8 + layer + 1, :]
        for layer in range(EDGE):
            row = start + REACH + layer
            send[row : row + 1, :] = edge[side, layer : layer + 1, :]
        send[start + SPAN : start + 32, :] = jnp.zeros((32 - SPAN, LANES), F32)


def widen_kernel(press, void, lower, upper, left, right, void_wide, press_wide, factor):
    for number, own, wide in ((0, void, void_wide), (1, press, press_wide)):
        for layer in range(WIDE):
            row = (number * WIDE + layer) * ROWS
            wide[layer, 0:8, :] = left[row : row + ROWS, :]
            wide[layer, 24:32, :] = right[row : row + ROWS, :]
            if layer < HALO:
                wide[layer, 8:24, :] = lower[number * HALO + layer, :, :]
            elif layer < HALO + EDGE:
                wide[layer, 8:24, :] = own[layer - HALO, :, :]
            else:
                wide[layer, 8:24, :] = upper[number * HALO + layer - HALO - EDGE, :, :]
    factor[0, :, :] = jnp.zeros((32, LANES), F32)
    factor[WIDE - 1, :, :] = jnp.zeros((32, LANES), F32)
    for layer in range(1, WIDE - 1):
        value = void_wide[layer, :, :]
        around = (
            void_wide[layer - 1, :, :] + void_wide[layer + 1, :, :]
            + row_up(value, 0.0) + row_down(value, 0.0) + lane_up(value) + lane_down(value)
        )
        outside = around <= 0.0
        factor[layer, :, :] = jnp.where(outside, 0.0, RELAXATION / jnp.where(outside, 1.0, around))


def relax_kernel(
    trial, void_wide, press_wide, factor, wide_div, sent_left, sent_right, left, right,
    velocity_out, pressure_out, press, known, first, second,
):
    start = SPAN * ROWS
    for layer in range(SPAN):
        row = layer * ROWS
        edge = slice(start + layer, start + layer + 1)
        middle = wide_div[layer, :, :]
        west = left[row : row + ROWS, :]
        east = right[row : row + ROWS, :]
        block = jnp.concatenate([west, middle, east], axis=0)
        place = lax.broadcasted_iota(jnp.int32, (32, LANES), 0)
        block = block + jnp.where(place == 7, sent_left[edge, :], 0.0)
        block = block - jnp.where(place == 8, left[edge, :], 0.0)
        block = block + jnp.where(place == 23, right[edge, :], 0.0)
        block = block - jnp.where(place == 24, sent_right[edge, :], 0.0)
        known[layer + 1, :, :] = -2.0 * factor[layer + 1, :, :] * block
    for layer in range(WIDE):
        first[layer, :, :] = void_wide[layer, :, :] * press_wide[layer, :, :]
    for sweep in range(1, SWEEPS + 1):
        source, target = (first, second) if sweep % 2 == 1 else (second, first)
        before = press_wide if sweep == 1 else press
        for layer in range(sweep, WIDE - sweep):
            value = source[layer, :, :]
            around = (
                source[layer - 1, :, :] + source[layer + 1, :, :]
                + pltpu.roll(value, 31, 0) + pltpu.roll(value, 1, 0) + lane_up(value) + lane_down(value)
            )
            new = (
                (1.0 - RELAXATION) * before[layer, :, :] + known[layer, :, :]
                + factor[layer, :, :] * around
            )
            press[layer, :, :] = new
            if sweep < SWEEPS:
                target[layer, :, :] = void_wide[layer, :, :] * new
    half_step = 0.5 * TIME_STEP
    inner = slice(8, 24)
    for layer in range(HALO, HALO + EDGE):
        here = press[layer, :, :]
        void = void_wide[layer, :, :]
        centre = here[inner, :]
        pressure_out[layer - HALO, :, :] = centre

        def gradient(ahead, void_ahead, behind, void_behind):
            return void_ahead * (ahead - here) + void_behind * (here - behind)

        pieces = (
            gradient(press[layer + 1, :, :], void_wide[layer + 1, :, :], press[layer - 1, :, :], void_wide[layer - 1, :, :]),
            gradient(pltpu.roll(here, 31, 0), pltpu.roll(void, 31, 0), pltpu.roll(here, 1, 0), pltpu.roll(void, 1, 0)),
            gradient(lane_up(here), lane_up(void), lane_down(here), lane_down(void)),
        )
        for axis_no in range(3):
            velocity_out[axis_no, layer - HALO, :, :] = (
                trial[axis_no, layer - HALO, :, :] - half_step * pieces[axis_no][inner, :]
            )


def to_next(value, axis, periodic):
    count = lax.axis_size(axis)
    pairs = [(i, i + 1) for i in range(count - 1)] + ([(count - 1, 0)] if periodic else [])
    return lax.ppermute(value, axis, pairs)


def to_previous(value, axis, periodic):
    count = lax.axis_size(axis)
    pairs = [(i + 1, i) for i in range(count - 1)] + ([(0, count - 1)] if periodic else [])
    return lax.ppermute(value, axis, pairs)


def per_device(
    velocity, pressure, void_fraction, history, remap_list, parcel_records, parcel_owner, parcel_cells
):
    cells = pressure.shape
    codes = remap_list.transpose(1, 2, 0).reshape(-1, remap_list.shape[0])
    fields = (velocity, history, pressure, void_fraction)
    bricks = (FIELDS * 32, LANES)
    up, down = call(pack_kernel, [bricks, bricks], (codes,) + fields, smem=(0,))
    brick_low = to_next(up, "gz", True)
    brick_high = to_previous(down, "gz", True)
    (outgoing,) = call(
        dispatch_kernel,
        [(OWNERS, 8, CAP)],
        (parcel_records, parcel_owner.reshape(32, 128), parcel_cells.reshape(32, 128)),
        scratch=(pltpu.VMEM((PARCELS // BLOCK * OWNERS, BLOCK), BF16), pltpu.VMEM((512, 2 * CAP), F32)),
    )
    layers = (2 * HALO + 3, EDGE, LANES)
    flow, latest, base, press, void, up, down = call(
        remap_kernel,
        [(3,) + cells, (3,) + cells, (3,) + cells, cells, cells, layers, layers],
        (codes,) + fields + (brick_low, brick_high),
        smem=(0,),
    )
    state_low = to_next(up, "gz", True)
    state_high = to_previous(down, "gz", True)
    arrived = lax.all_to_all(outgoing, "gz", split_axis=0, concat_axis=0, tiled=True)
    rows = (2 * WIDE * ROWS + 3 * EDGE, LANES)
    right, left = call(pack_rows_kernel, [rows, rows], (flow, press, void, state_low, state_high))
    state_left = to_next(right, "gx", False)
    state_right = to_previous(left, "gx", False)
    (deposit,) = call(
        deposit_kernel, [(4,) + cells], (arrived,), scratch=(pltpu.VMEM((1024, 2 * LANES), F32),)
    )
    layers = (REACH + 2, EDGE, LANES)
    new_history, trial, div, up, down, edge = call(
        rate_kernel,
        [(2, 3) + cells, (3,) + cells, cells, layers, layers, (2, EDGE, LANES)],
        (flow, latest, base, void, state_low, state_high, state_left, state_right, deposit),
        scratch=(pltpu.VMEM(cells, F32),),
    )
    div_low = to_next(up, "gz", True)
    div_high = to_previous(down, "gz", True)
    wide = (WIDE, 32, LANES)
    void_wide, press_wide, factor = call(
        widen_kernel, [wide, wide, wide], (press, void, state_low, state_high, state_left, state_right)
    )
    rows = (SPAN * ROWS + 32, LANES)
    wide_div, right, left = call(
        pack_div_kernel,
        [(SPAN, EDGE, LANES), rows, rows],
        (div, down, up, edge, div_low, div_high),
    )
    div_left = to_next(right, "gx", False)
    div_right = to_previous(left, "gx", False)
    new_velocity, new_pressure = call(
        relax_kernel,
        [(3,) + cells, cells],
        (trial, void_wide, press_wide, factor, wide_div, left, right, div_left, div_right),
        scratch=(pltpu.VMEM(wide, F32), pltpu.VMEM(wide, F32), pltpu.VMEM(wide, F32), pltpu.VMEM(wide, F32)),
    )
    return new_velocity, new_pressure, new_history


def solution(mesh):
    return jax.shard_map(
        per_device,
        mesh=mesh,
        in_specs=(
            P(None, "gz", "gx", None),
            P("gz", "gx", None),
            P("gz", "gx", None),
            P(None, None, "gz", "gx", None),
            P(),
            P(None, ("gz", "gx")),
            P(("gz", "gx"), None),
            P(("gz", "gx")),
        ),
        out_specs=(P(None, "gz", "gx", None), P("gz", "gx", None), P(None, None, "gz", "gx", None)),
        check_vma=False,
    )
```

profile of v0, /device:TPU:1, one launch (start us, length us, event | category | flops | bytes accessed | tf_op | source)
XLA Modules:
  0.0 87.3 jit_solution(13023422437861727317)
XLA Ops:
  0.6 0.0 copy-start
  0.6 1.1 %copy-done = f32[2,3,16,16,128]{4,3,2,1,0:T(8,128)S(1)} copy-done((f32[2,3,16,16,128]{4,3,2,1,0:T(8,128)S(1)}, f32[2,3,16,16,128]{4,3,2,1,0:T(8,128)}, u32[]{:S(2)}) %copy-start) | copy-done | bytes 786456
  1.8 0.0 copy-start.2
  1.8 1.0 %copy-done.2 = f32[3,16,16,128]{3,2,1,0:T(8,128)S(1)} copy-done((f32[3,16,16,128]{3,2,1,0:T(8,128)S(1)}, f32[3,16,16,128]{3,2,1,0:T(8,128)}, u32[]{:S(2)}) %copy-start.2) | copy-done | bytes 393240
  2.8 0.0 copy-start.4
  2.8 0.9 %copy-done.4 = f32[16,16,128]{2,1,0:T(8,128)S(1)} copy-done((f32[16,16,128]{2,1,0:T(8,128)S(1)}, f32[16,16,128]{2,1,0:T(8,128)}, u32[]{:S(2)}) %copy-start.4) | copy-done | bytes 131096
  3.7 0.0 copy-start.6
  3.7 0.9 %copy-done.6 = f32[16,16,128]{2,1,0:T(8,128)S(1)} copy-done((f32[16,16,128]{2,1,0:T(8,128)S(1)}, f32[16,16,128]{2,1,0:T(8,128)}, u32[]{:S(2)}) %copy-start.6) | copy-done | bytes 131096
  4.6 0.0 copy-start.9
  4.6 0.7 copy-done.9
  5.3 0.0 copy-start.8
  5.3 0.0 copy-start.11
  5.3 0.0 copy-start.12
  5.3 0.0 copy-start.3
  5.3 1.7 %shard_map.103 = (f32[352,128]{1,0:T(8,128)S(1)}, f32[352,128]{1,0:T(8,128)S(1)}) custom-call(s32[32,64]{1,0:T(8,128)S(1)} %bitcast.5, f32[3,16,16,128]{3,2,1,0:T(8,128)S(1)} %copy-done.2, f32[2,3,16,16,128]{4,3,2,1,0:T(8,128)S(1)} %copy-done, f32[16,16,128]{2,1,0:T(8,128)S(1)} %copy-done.4, f32[16,16,128]{2,1,0:T(8,128)S(1)} %copy-done.6), custom_call_target="tpu_custom_call" | custom-call | tf_op jit(solution)/shard_map/pallas_call | solution.py:42
  7.0 0.0 copy-start.1
  7.0 3.8 %collective-permute-start = (f32[352,128]{1,0:T(8,128)S(1)}, f32[352,128]{1,0:T(8,128)S(1)}, u32[]{:S(2)}, u32[]{:S(2)}) collective-permute-start(f32[352,128]{1,0:T(8,128)S(1)} %get-tuple-element.28), channel_id=1, source_target_pairs={{0,4},{4,8},{8,12},{12,16},{16,20},{20,24},{24,28},{28,32},{32,36}... | collective-permute-start | bytes 540680 | tf_op jit(solution)/shard_map/ppermute | solution.py:491
  10.8 7.6 %collective-permute-start.1 = (f32[352,128]{1,0:T(8,128)S(1)}, f32[352,128]{1,0:T(8,128)S(1)}, u32[]{:S(2)}, u32[]{:S(2)}) collective-permute-start(f32[352,128]{1,0:T(8,128)S(1)} %get-tuple-element.29), channel_id=1, source_target_pairs={{4,0},{8,4},{12,8},{16,12},{20,16},{24,20},{28,24},{32,28},{36,32}... | collective-permute-start | bytes 540680 | tf_op jit(solution)/shard_map/ppermute | solution.py:497
  18.4 0.0 copy-done.8
  18.4 0.0 copy-done.11
  18.4 0.0 copy-done.12
  18.4 2.8 %shard_map.106 = f32[64,8,128]{2,1,0:T(8,128)} custom-call(f32[16,4096]{1,0:T(8,128)S(1)} %copy-done.8, s32[32,128]{1,0:T(8,128)S(1)} %bitcast.7, s32[32,128]{1,0:T(8,128)S(1)} %bitcast.8), custom_call_target="tpu_custom_call" | custom-call | tf_op jit(solution)/shard_map/pallas_call | solution.py:42
  21.1 0.0 copy-start.5
  21.1 0.0 copy-start.7
  21.2 0.0 copy-start.10
  21.2 6.9 %all-to-all-start = ((f32[64,8,128]{2,1,0:T(8,128)}), f32[64,8,128]{2,1,0:T(8,128)S(1)}, u32[]{:S(2)}, u32[]{:S(2)}) async-start(f32[64,8,128]{2,1,0:T(8,128)} %shard_map.106), calls=%async_computation | async-start | bytes 524288 | tf_op jit(solution)/shard_map/all_to_all | solution.py:525
  28.1 0.0 collective-permute-done.lower
  28.1 0.0 collective-permute-done.1.upper
  28.1 0.0 copy-done.3
  28.1 0.0 copy-done.1
  28.1 0.0 copy-done.5
  28.1 0.0 copy-done.7
  28.1 0.0 copy-done.10
  28.1 3.0 %shard_map.104 = (f32[3,16,16,128]{3,2,1,0:T(8,128)S(1)}, f32[3,16,16,128]{3,2,1,0:T(8,128)S(1)}, f32[3,16,16,128]{3,2,1,0:T(8,128)S(1)}, f32[16,16,128]{2,1,0:T...) custom-call(s32[32,64]{1,0:T(8,128)S(1)} %bitcast.6, ...), custom_call_target="tpu_custom_call" | custom-call | tf_op jit(solution)/shard_map/pallas_call | solution.py:42
  31.1 2.6 %collective-permute-start.2 = (f32[17,16,128]{2,1,0:T(8,128)S(1)}, f32[17,16,128]{2,1,0:T(8,128)S(1)}, u32[]{:S(2)}, u32[]{:S(2)}) collective-permute-start(f32[17,16,128]{2,1,0:T(8,128)S(1)} %get-tuple-element.34), channel_id=1, source_target_pairs={{0,4},{4,8},{8,12},{12,16},{16,20},{20,24},{24,28},{28,32},{32,36}... | collective-permute-start | bytes 417800 | tf_op jit(solution)/shard_map/ppermute | solution.py:491
  33.7 4.7 %collective-permute-start.3 = (f32[17,16,128]{2,1,0:T(8,128)S(1)}, f32[17,16,128]{2,1,0:T(8,128)S(1)}, u32[]{:S(2)}, u32[]{:S(2)}) collective-permute-start(f32[17,16,128]{2,1,0:T(8,128)S(1)} %get-tuple-element.35), channel_id=1, source_target_pairs={{4,0},{8,4},{12,8},{16,12},{20,16},{24,20},{28,24},{32,28},{36,32}... | collective-permute-start | bytes 417800 | tf_op jit(solution)/shard_map/ppermute | solution.py:497
  38.4 6.0 %collective-permute-done.2.lower = f32[17,16,128]{2,1,0:T(8,128)S(1)} collective-permute-done((f32[17,16,128]{2,1,0:T(8,128)S(1)}, f32[17,16,128]{2,1,0:T(8,128)S(1)}, u32[]{:S(2)}, u32[]{:S(2)}) %collective-permute-start.2) | collective-permute-done | bytes 139296 | tf_op jit(solution)/shard_map/ppermute | solution.py:491
  44.4 0.0 collective-permute-done.3.upper
  44.4 0.1 shard_map.105
  44.5 3.8 %collective-permute-start.4 = (f32[528,128]{1,0:T(8,128)S(1)}, f32[528,128]{1,0:T(8,128)S(1)}, u32[]{:S(2)}, u32[]{:S(2)}) collective-permute-start(f32[528,128]{1,0:T(8,128)S(1)} %get-tuple-element.37), channel_id=1, source_target_pairs={{0,1},{1,2},{2,3},{4,5},{5,6},{6,7},{8,9},{9,10},{10,11},{12,13},{... | collective-permute-start | bytes 811016 | tf_op jit(solution)/shard_map/ppermute | solution.py:491
  48.3 1.9 %collective-permute-start.5 = (f32[528,128]{1,0:T(8,128)S(1)}, f32[528,128]{1,0:T(8,128)S(1)}, u32[]{:S(2)}, u32[]{:S(2)}) collective-permute-start(f32[528,128]{1,0:T(8,128)S(1)} %get-tuple-element.38), channel_id=1, source_target_pairs={{1,0},{2,1},{3,2},{5,4},{6,5},{7,6},{9,8},{10,9},{11,10},{13,12},{... | collective-permute-start | bytes 811016 | tf_op jit(solution)/shard_map/ppermute | solution.py:497
  50.2 0.0 all-to-all-done.arrived
  50.2 13.0 %shard_map.107.deposit = f32[4,16,16,128]{3,2,1,0:T(8,128)S(1)} custom-call(f32[64,8,128]{2,1,0:T(8,128)S(1)} %all-to-all-done.arrived), custom_call_target="tpu_custom_call" | custom-call | tf_op jit(solution)/shard_map/pallas_call | solution.py:42
  63.3 0.0 collective-permute-done.4.left
  63.3 0.0 collective-permute-done.5.right
  63.3 1.9 %shard_map.108 = (f32[2,3,16,16,128]{4,3,2,1,0:T(8,128)}, f32[3,16,16,128]{3,2,1,0:T(8,128)S(1)}, f32[16,16,128]{2,1,0:T(8,128)S(1)}, f32[8,16,128]{2,1,0:T(8,12...) custom-call(f32[3,16,16,128]{3,2,1,0:T(8,128)S(1)} %get-tuple-element.30.flow, ...), custom_call_target="tpu_custom_call" | custom-call | tf_op jit(solution)/shard_map/pallas_call | solution.py:42
  65.2 0.6 collective-permute-start.6
  65.8 6.6 %collective-permute-start.7 = (f32[8,16,128]{2,1,0:T(8,128)S(1)}, f32[8,16,128]{2,1,0:T(8,128)S(1)}, u32[]{:S(2)}, u32[]{:S(2)}) collective-permute-start(f32[8,16,128]{2,1,0:T(8,128)S(1)} %get-tuple-element.44.sent_lower), channel_id=1, source_target_pairs={{4,0},{8,4},{12,8},{16,12},{20,16},{24,20},{28,24},{32,28},{36,32}... | collective-permute-start | bytes 196616 | tf_op jit(solution)/shard_map/ppermute | solution.py:497
  72.4 1.6 %collective-permute-done.6.lower = f32[8,16,128]{2,1,0:T(8,128)S(1)} collective-permute-done((f32[8,16,128]{2,1,0:T(8,128)S(1)}, f32[8,16,128]{2,1,0:T(8,128)S(1)}, u32[]{:S(2)}, u32[]{:S(2)}) %collective-permute-start.6) | collective-permute-done | bytes 65568 | tf_op jit(solution)/shard_map/ppermute | solution.py:491
  74.1 0.0 collective-permute-done.7.upper
  74.1 4.8 %collective-permute-start.8 = (f32[256,128]{1,0:T(8,128)S(1)}, f32[256,128]{1,0:T(8,128)S(1)}, u32[]{:S(2)}, u32[]{:S(2)}) collective-permute-start(f32[256,128]{1,0:T(8,128)S(1)} %get-tuple-element.49.sent_right), channel_id=1, source_target_pairs={{0,1},{1,2},{2,3},{4,5},{5,6},{6,7},{8,9},{9,10},{10,11},{12,13},{... | collective-permute-start | bytes 393224 | tf_op jit(solution)/shard_map/ppermute | solution.py:491
  78.9 1.9 %collective-permute-start.9 = (f32[256,128]{1,0:T(8,128)S(1)}, f32[256,128]{1,0:T(8,128)S(1)}, u32[]{:S(2)}, u32[]{:S(2)}) collective-permute-start(f32[256,128]{1,0:T(8,128)S(1)} %get-tuple-element.48.sent_left), channel_id=1, source_target_pairs={{1,0},{2,1},{3,2},{5,4},{6,5},{7,6},{9,8},{10,9},{11,10},{13,12},{... | collective-permute-start | bytes 393224 | tf_op jit(solution)/shard_map/ppermute | solution.py:497
  80.8 0.4 shard_map.109
  81.2 0.0 collective-permute-done.8.left
  81.2 4.0 %collective-permute-done.9.right = f32[256,128]{1,0:T(8,128)S(1)} collective-permute-done((f32[256,128]{1,0:T(8,128)S(1)}, f32[256,128]{1,0:T(8,128)S(1)}, u32[]{:S(2)}, u32[]{:S(2)}) %collective-permute-start.9) | collective-permute-done | bytes 131104 | tf_op jit(solution)/shard_map/ppermute | solution.py:497
  85.2 2.1 %shard_map.111 = (f32[3,16,16,128]{3,2,1,0:T(8,128)}, f32[16,16,128]{2,1,0:T(8,128)}) custom-call(f32[3,16,16,128]{3,2,1,0:T(8,128)S(1)} %get-tuple-element.39.trial, f32[30,32,128]{2,1,0:T(8,128)S(1)} %get-tuple-element.40.void_wide, f32[30,32,128]{2,1,0:T(8,128)S(1)} %get-tuple-element.41.press_wide, f32[30,32,128]{2,1,0:T(8,128)S(1)} %get-tuple-element.42.factor, ...), custom_call_target="tpu_custom_call" | custom-call | tf_op jit(solution)/shard_map/pallas_call | solution.py:42
  (1 shorter events, 0.0 us)
Async XLA Ops:
  0.6 1.1 %copy-start = (f32[2,3,16,16,128]{4,3,2,1,0:T(8,128)S(1)}, f32[2,3,16,16,128]{4,3,2,1,0:T(8,128)}, u32[]{:S(2)}) copy-start(f32[2,3,16,16,128]{4,3,2,1,0:T(8,128)} %history.3) | copy-start | bytes 2359300
  1.8 1.0 %copy-start.2 = (f32[3,16,16,128]{3,2,1,0:T(8,128)S(1)}, f32[3,16,16,128]{3,2,1,0:T(8,128)}, u32[]{:S(2)}) copy-start(f32[3,16,16,128]{3,2,1,0:T(8,128)} %velocity.3) | copy-start | bytes 1179652
  2.8 0.9 %copy-start.4 = (f32[16,16,128]{2,1,0:T(8,128)S(1)}, f32[16,16,128]{2,1,0:T(8,128)}, u32[]{:S(2)}) copy-start(f32[16,16,128]{2,1,0:T(8,128)} %pressure.3) | copy-start | bytes 393220
  3.7 0.9 %copy-start.6 = (f32[16,16,128]{2,1,0:T(8,128)S(1)}, f32[16,16,128]{2,1,0:T(8,128)}, u32[]{:S(2)}) copy-start(f32[16,16,128]{2,1,0:T(8,128)} %void.3) | copy-start | bytes 393220
  4.6 0.7 copy-start.9
  5.3 13.1 %copy-start.8 = (f32[16,4096]{1,0:T(8,128)S(1)}, f32[16,4096]{1,0:T(8,128)}, u32[]{:S(2)}) copy-start(f32[16,4096]{1,0:T(8,128)} %records.1) | copy-start | bytes 786436
  5.3 13.1 %copy-start.11 = (s32[4096,1]{0,1:T(1,128)S(1)}, s32[4096,1]{0,1:T(1,128)}, u32[]{:S(2)}) copy-start(s32[4096,1]{0,1:T(1,128)} %param.14) | copy-start | bytes 49156
  5.3 13.1 %copy-start.12 = (s32[4096]{0:T(1024)S(1)}, s32[4096]{0:T(1024)}, u32[]{:S(2)}) copy-start(s32[4096]{0:T(1024)} %param.15) | copy-start | bytes 49156
  5.3 22.8 %copy-start.3 = (f32[3,16,16,128]{3,2,1,0:T(8,128)S(1)}, f32[3,16,16,128]{3,2,1,0:T(8,128)}, u32[]{:S(2)}) copy-start(f32[3,16,16,128]{3,2,1,0:T(8,128)} %velocity.3) | copy-start | bytes 1179652
  7.0 21.1 %copy-start.1 = (f32[2,3,16,16,128]{4,3,2,1,0:T(8,128)S(1)}, f32[2,3,16,16,128]{4,3,2,1,0:T(8,128)}, u32[]{:S(2)}) copy-start(f32[2,3,16,16,128]{4,3,2,1,0:T(8,128)} %history.3) | copy-start | bytes 2359300
  7.0 21.1 %collective-permute-start = (f32[352,128]{1,0:T(8,128)S(1)}, f32[352,128]{1,0:T(8,128)S(1)}, u32[]{:S(2)}, u32[]{:S(2)}) collective-permute-start(f32[352,128]{1,0:T(8,128)S(1)} %get-tuple-element.28), channel_id=1, source_target_pairs={{0,4},{4,8},{8,12},{12,16},{16,20},{20,24},{24,28},{28,32},{32,36}... | collective-permute-start | bytes 540680 | tf_op jit(solution)/shard_map/ppermute | solution.py:491
  10.8 17.3 %collective-permute-start.1 = (f32[352,128]{1,0:T(8,128)S(1)}, f32[352,128]{1,0:T(8,128)S(1)}, u32[]{:S(2)}, u32[]{:S(2)}) collective-permute-start(f32[352,128]{1,0:T(8,128)S(1)} %get-tuple-element.29), channel_id=1, source_target_pairs={{4,0},{8,4},{12,8},{16,12},{20,16},{24,20},{28,24},{32,28},{36,32}... | collective-permute-start | bytes 540680 | tf_op jit(solution)/shard_map/ppermute | solution.py:497
  21.1 7.0 %copy-start.5 = (f32[16,16,128]{2,1,0:T(8,128)S(1)}, f32[16,16,128]{2,1,0:T(8,128)}, u32[]{:S(2)}) copy-start(f32[16,16,128]{2,1,0:T(8,128)} %pressure.3) | copy-start | bytes 393220
  21.1 7.0 %copy-start.7 = (f32[16,16,128]{2,1,0:T(8,128)S(1)}, f32[16,16,128]{2,1,0:T(8,128)}, u32[]{:S(2)}) copy-start(f32[16,16,128]{2,1,0:T(8,128)} %void.3) | copy-start | bytes 393220
  21.2 7.0 %copy-start.10 = (s32[64,4,8]{0,2,1:T(8,128)S(1)}, s32[64,4,8]{0,2,1:T(8,128)}, u32[]{:S(2)}) copy-start(s32[64,4,8]{0,2,1:T(8,128)} %param.12) | copy-start | bytes 24580
  21.2 29.1 %all-to-all-start = ((f32[64,8,128]{2,1,0:T(8,128)}), f32[64,8,128]{2,1,0:T(8,128)S(1)}, u32[]{:S(2)}, u32[]{:S(2)}) async-start(f32[64,8,128]{2,1,0:T(8,128)} %shard_map.106), calls=%async_computation | async-start | bytes 524288 | tf_op jit(solution)/shard_map/all_to_all | solution.py:525
  31.1 13.3 %collective-permute-start.2 = (f32[17,16,128]{2,1,0:T(8,128)S(1)}, f32[17,16,128]{2,1,0:T(8,128)S(1)}, u32[]{:S(2)}, u32[]{:S(2)}) collective-permute-start(f32[17,16,128]{2,1,0:T(8,128)S(1)} %get-tuple-element.34), channel_id=1, source_target_pairs={{0,4},{4,8},{8,12},{12,16},{16,20},{20,24},{24,28},{28,32},{32,36}... | collective-permute-start | bytes 417800 | tf_op jit(solution)/shard_map/ppermute | solution.py:491
  33.7 10.7 %collective-permute-start.3 = (f32[17,16,128]{2,1,0:T(8,128)S(1)}, f32[17,16,128]{2,1,0:T(8,128)S(1)}, u32[]{:S(2)}, u32[]{:S(2)}) collective-permute-start(f32[17,16,128]{2,1,0:T(8,128)S(1)} %get-tuple-element.35), channel_id=1, source_target_pairs={{4,0},{8,4},{12,8},{16,12},{20,16},{24,20},{28,24},{32,28},{36,32}... | collective-permute-start | bytes 417800 | tf_op jit(solution)/shard_map/ppermute | solution.py:497
  44.5 18.8 %collective-permute-start.4 = (f32[528,128]{1,0:T(8,128)S(1)}, f32[528,128]{1,0:T(8,128)S(1)}, u32[]{:S(2)}, u32[]{:S(2)}) collective-permute-start(f32[528,128]{1,0:T(8,128)S(1)} %get-tuple-element.37), channel_id=1, source_target_pairs={{0,1},{1,2},{2,3},{4,5},{5,6},{6,7},{8,9},{9,10},{10,11},{12,13},{... | collective-permute-start | bytes 811016 | tf_op jit(solution)/shard_map/ppermute | solution.py:491
  48.3 15.0 %collective-permute-start.5 = (f32[528,128]{1,0:T(8,128)S(1)}, f32[528,128]{1,0:T(8,128)S(1)}, u32[]{:S(2)}, u32[]{:S(2)}) collective-permute-start(f32[528,128]{1,0:T(8,128)S(1)} %get-tuple-element.38), channel_id=1, source_target_pairs={{1,0},{2,1},{3,2},{5,4},{6,5},{7,6},{9,8},{10,9},{11,10},{13,12},{... | collective-permute-start | bytes 811016 | tf_op jit(solution)/shard_map/ppermute | solution.py:497
  65.2 8.8 %collective-permute-start.6 = (f32[8,16,128]{2,1,0:T(8,128)S(1)}, f32[8,16,128]{2,1,0:T(8,128)S(1)}, u32[]{:S(2)}, u32[]{:S(2)}) collective-permute-start(f32[8,16,128]{2,1,0:T(8,128)S(1)} %get-tuple-element.45.sent_upper), channel_id=1, source_target_pairs={{0,4},{4,8},{8,12},{12,16},{16,20},{20,24},{24,28},{28,32},{32,36}... | collective-permute-start | bytes 196616 | tf_op jit(solution)/shard_map/ppermute | solution.py:491
  65.8 8.3 %collective-permute-start.7 = (f32[8,16,128]{2,1,0:T(8,128)S(1)}, f32[8,16,128]{2,1,0:T(8,128)S(1)}, u32[]{:S(2)}, u32[]{:S(2)}) collective-permute-start(f32[8,16,128]{2,1,0:T(8,128)S(1)} %get-tuple-element.44.sent_lower), channel_id=1, source_target_pairs={{4,0},{8,4},{12,8},{16,12},{20,16},{24,20},{28,24},{32,28},{36,32}... | collective-permute-start | bytes 196616 | tf_op jit(solution)/shard_map/ppermute | solution.py:497
  74.1 7.1 %collective-permute-start.8 = (f32[256,128]{1,0:T(8,128)S(1)}, f32[256,128]{1,0:T(8,128)S(1)}, u32[]{:S(2)}, u32[]{:S(2)}) collective-permute-start(f32[256,128]{1,0:T(8,128)S(1)} %get-tuple-element.49.sent_right), channel_id=1, source_target_pairs={{0,1},{1,2},{2,3},{4,5},{5,6},{6,7},{8,9},{9,10},{10,11},{12,13},{... | collective-permute-start | bytes 393224 | tf_op jit(solution)/shard_map/ppermute | solution.py:491
  78.9 6.3 %collective-permute-start.9 = (f32[256,128]{1,0:T(8,128)S(1)}, f32[256,128]{1,0:T(8,128)S(1)}, u32[]{:S(2)}, u32[]{:S(2)}) collective-permute-start(f32[256,128]{1,0:T(8,128)S(1)} %get-tuple-element.48.sent_left), channel_id=1, source_target_pairs={{1,0},{2,1},{3,2},{5,4},{6,5},{7,6},{9,8},{10,9},{11,10},{13,12},{... | collective-permute-start | bytes 393224 | tf_op jit(solution)/shard_map/ppermute | solution.py:497
where the time goes:
time: 87.7 us; the launch traced here: 87.3 us
  starting transfers between devices  45.2 us (52%)
  Pallas kernels  25 us (29%)
  waiting for transfers between devices  11.7 us (13%)
  local copies, waits for them, and re-layouts  4.68 us (5%)
    pallas_call x9, Pallas kernels, call(): pl.pallas_call(kernel, out_shape=[jax.ShapeDtypeStruct(shape, F32) for sh...  25 us
    ppermute x5, starting transfers between devices, to_previous(): return lax.ppermute(value, axis, pairs)  22.7 us
    ppermute x5, starting transfers between devices, to_next(): return lax.ppermute(value, axis, pairs)  15.6 us
    ppermute x5, waiting for transfers between devices, to_next(): return lax.ppermute(value, axis, pairs)  7.67 us
    all_to_all x1, starting transfers between devices, per_device(): lax.all_to_all(outgoing, 'gz', split_axis=0, concat_axis=0, tiled=True)  6.89 us
    unnamed x26, local copies, waits for them, and re-layouts  4.68 us
    ppermute x5, waiting for transfers between devices, to_previous(): return lax.ppermute(value, axis, pairs)  3.98 us
  transfers between devices with their start and end apart: 11, of which 3 were waited for; matrix products, arithmetic and copies ran while one was open for 0% of the time, Pallas kernels for 22%

commit v1 on v0

--- a/solution.py
+++ b/solution.py
@@ -28,21 +28,22 @@
 CAP = 128
 PARCELS = 4096
 BLOCK = 256
+STEP = 4
 VMEM_LIMIT = 48 * 1024 * 1024
 
 F32 = jnp.float32
 BF16 = jnp.bfloat16
 
 
-def call(kernel, outs, args, smem=(), scratch=()):
-    specs = [
-        pl.BlockSpec(memory_space=pltpu.SMEM if number in smem else pltpu.VMEM)
-        for number in range(len(args))
-    ]
+def call(kernel, outs, args, spaces=None, scratch=()):
+    spaces = spaces or {}
+    shapes = [out if isinstance(out, jax.ShapeDtypeStruct) else jax.ShapeDtypeStruct(out, F32) for out in outs]
     return pl.pallas_call(
         kernel,
-        out_shape=[jax.ShapeDtypeStruct(shape, F32) for shape in outs],
-        in_specs=specs,
+        out_shape=shapes,
+        in_specs=[
+            pl.BlockSpec(memory_space=spaces.get(number, pltpu.VMEM)) for number in range(len(args))
+        ],
         out_specs=[pl.BlockSpec(memory_space=pltpu.VMEM) for _ in outs],
         scratch_shapes=list(scratch),
         compiler_params=pltpu.CompilerParams(vmem_limit_bytes=VMEM_LIMIT),
@@ -68,7 +69,7 @@
     return (pressure if field == 9 else void)[layer, rows, :]
 
 
-def pack_kernel(codes, velocity, history, pressure, void, to_upper, to_lower):
+def pack_bricks(codes, refs, to_upper, to_lower, code_out):
     cycle = lax.axis_index("gz")
     line = lax.axis_index("gx")
     size = lax.axis_size("gz")
@@ -76,16 +77,18 @@
     lower = lax.rem(cycle + size - 1, size)
     slot_up = jnp.int32(0)
     slot_down = jnp.int32(0)
+    lane = lane_of()
+    group = lane // BRICK
+    code_of = jnp.zeros((ROWS, LANES), jnp.int32)
     for brick in range(BRICKS):
         code = codes[line * BRICKS + brick, upper]
         slot_up = slot_up + jnp.where(code < BRICKS, code, 0)
         code = codes[line * BRICKS + brick, lower]
         slot_down = slot_down + jnp.where(code >= 2 * BRICKS, code - 2 * BRICKS, 0)
-    lane = lane_of()
-    group = lane // BRICK
+        code_of = jnp.where(group == brick, codes[line * BRICKS + brick, cycle], code_of)
+    code_out[...] = code_of
     index_up = slot_up * BRICK + lane % BRICK
     index_down = slot_down * BRICK + lane % BRICK
-    refs = (velocity, history, pressure, void)
     for field in range(FIELDS):
         for part in range(4):
             up = jnp.zeros((ROWS, LANES), F32)
@@ -99,53 +102,81 @@
             to_lower[row : row + ROWS, :] = down
 
 
-def remap_kernel(
-    codes, velocity, history, pressure, void, lower, upper,
-    flow_out, latest_out, base_out, press_out, void_out, to_upper, to_lower,
-):
-    cycle = lax.axis_index("gz")
-    line = lax.axis_index("gx")
+def copied(sources, targets, arrivals):
+    return [
+        pltpu.make_async_copy(source, target, arrivals.at[number])
+        for number, (source, target) in enumerate(zip(sources, targets))
+    ]
+
+
+def pack_kernel(*refs):
+    sources, (to_upper, to_lower, code_out), held, arrivals = refs[:5], refs[5:8], refs[8:13], refs[13]
+    copies = copied(sources, held, arrivals)
+    for copy in copies:
+        copy.start()
+    for copy in copies:
+        copy.wait()
+    pack_bricks(held[0], held[1:], to_upper, to_lower, code_out)
+
+
+def remapper(code_ref, refs, lower, upper):
     lane = lane_of()
-    group = lane // BRICK
-    code_of = jnp.zeros((ROWS, LANES), jnp.int32)
-    for brick in range(BRICKS):
-        code_of = jnp.where(group == brick, codes[line * BRICKS + brick, cycle], code_of)
+    code_of = code_ref[...]
     from_lower = code_of < BRICKS
     from_upper = code_of >= 2 * BRICKS
     index_own = (code_of % BRICKS) * BRICK + lane % BRICK
-    refs = (velocity, history, pressure, void)
-    for tile in range(32):
+
+    def moved(field, tile):
         part, place = tile // 8, tile % 8
         index_in = place * BRICK + lane % BRICK
-        layer, half = tile // 2, tile % 2
-        rows = slice(half * ROWS, (half + 1) * ROWS)
-        moved = []
-        for field in range(FIELDS):
-            row = (field * 4 + part) * ROWS
-            own = take(field_block(refs, field, tile), index_own)
-            low = take(lower[row : row + ROWS, :], index_in)
-            high = take(upper[row : row + ROWS, :], index_in)
-            moved.append(jnp.where(from_lower, low, jnp.where(from_upper, high, own)))
-        press, void_new = moved[9], moved[10]
+        row = (field * 4 + part) * ROWS
+        own = take(field_block(refs, field, tile), index_own)
+        low = take(lower[row : row + ROWS, :], index_in)
+        high = take(upper[row : row + ROWS, :], index_in)
+        return jnp.where(from_lower, low, jnp.where(from_upper, high, own))
+
+    return moved
+
+
+def tile_at(tile):
+    half = tile % 2
+    return tile // 2, slice(half * ROWS, (half + 1) * ROWS)
+
+
+def remap_first_kernel(
+    codes, velocity, history, pressure, void, lower, upper, press_out, void_out, to_upper, to_lower
+):
+    moved = remapper(codes, (velocity, history, pressure, void), lower, upper)
+    for tile in range(32):
+        layer, rows = tile_at(tile)
+        press, void_new = moved(9, tile), moved(10, tile)
         press_out[layer, rows, :] = press
         void_out[layer, rows, :] = void_new
-        for axis_no in range(3):
-            flow, latest, older = moved[axis_no], moved[3 + axis_no], moved[6 + axis_no]
-            flow_out[axis_no, layer, rows, :] = flow
-            latest_out[axis_no, layer, rows, :] = latest
-            base_out[axis_no, layer, rows, :] = flow + TIME_STEP * (
-                WEIGHT_OLDER * older - WEIGHT_LAST * latest
-            )
-            if layer == 0:
-                to_lower[2 * HALO + axis_no, rows, :] = void_new * flow
-            if layer == EDGE - 1:
-                to_upper[2 * HALO + axis_no, rows, :] = void_new * flow
+        for send, edge in ((to_lower, 0), (to_upper, EDGE - 1)):
+            if layer == edge:
+                for axis_no in range(3):
+                    send[2 * HALO + axis_no, rows, :] = void_new * moved(axis_no, tile)
         if layer < HALO:
             to_lower[layer, rows, :] = void_new
             to_lower[HALO + layer, rows, :] = press
         if layer >= EDGE - HALO:
             to_upper[layer - EDGE + HALO, rows, :] = void_new
             to_upper[2 * HALO + layer - EDGE, rows, :] = press
+
+
+def remap_rest_kernel(
+    codes, velocity, history, pressure, void, lower, upper, flow_out, latest_out, base_out
+):
+    moved = remapper(codes, (velocity, history, pressure, void), lower, upper)
+    for tile in range(32):
+        layer, rows = tile_at(tile)
+        for axis_no in range(3):
+            flow, latest, older = [moved(axis_no + kind, tile) for kind in (0, 3, 6)]
+            flow_out[axis_no, layer, rows, :] = flow
+            latest_out[axis_no, layer, rows, :] = latest
+            base_out[axis_no, layer, rows, :] = flow + TIME_STEP * (
+                WEIGHT_OLDER * older - WEIGHT_LAST * latest
+            )
 
 
 def pack_rows_kernel(flow, press, void, lower, upper, to_right, to_left):
@@ -231,40 +262,39 @@
         out[owner, :, :] = total[row : row + 8, lanes] + total[row + 8 : row + 16, lanes]
 
 
-def deposit_kernel(arrived, out, total):
-    step = 4
-    width = step * CAP
-    iota_major = lax.broadcasted_iota(jnp.int32, (128, width), 0).astype(F32).astype(BF16)
-    iota_minor = lax.broadcasted_iota(jnp.int32, (256, width), 0).astype(F32).astype(BF16)
-    total[...] = jnp.zeros_like(total)
-    zero = jnp.zeros((128, width), BF16)
-
-    def body(number, carry):
-        def row_of(channel):
-            return jnp.concatenate(
-                [arrived[number * step + source, channel : channel + 1, :] for source in range(step)], axis=1
-            )
-
-        major = jnp.broadcast_to(row_of(4), (128, width)).astype(BF16)
-        minor = jnp.broadcast_to(row_of(5), (256, width)).astype(BF16)
-        placed = jnp.where(minor == iota_minor, jnp.ones((256, width), BF16), jnp.zeros((256, width), BF16))
-        here = major == iota_major
-        for channel in range(4):
-            value = row_of(channel)
-            coarse = value.astype(BF16).astype(F32)
-            for part, piece in ((0, coarse), (1, value - coarse)):
-                spread = jnp.where(here, jnp.broadcast_to(piece, (128, width)).astype(BF16), zero)
-                row = (channel * 2 + part) * 128
-                total[row : row + 128, :] += lax.dot_general(spread, placed, NT, preferred_element_type=F32)
-        return carry
-
-    lax.fori_loop(0, OWNERS // step, body, 0)
+def deposit_kernel(arrived, out, total, spread):
+    iota_major = lax.broadcasted_iota(jnp.int32, (128, CAP), 0).astype(F32).astype(BF16)
+    iota_minor = lax.broadcasted_iota(jnp.int32, (2 * LANES, CAP), 0).astype(F32).astype(BF16)
+    zero = jnp.zeros((128, CAP), BF16)
+    for start in range(0, OWNERS, STEP):
+        placed = []
+        for place in range(STEP):
+            slots = arrived[start + place, :, :]
+            lanes = slice(place * CAP, (place + 1) * CAP)
+            here = jnp.broadcast_to(slots[4:5, :], (128, CAP)).astype(BF16) == iota_major
+            for channel in range(4):
+                value = slots[channel : channel + 1, :]
+                coarse = value.astype(BF16).astype(F32)
+                for part, piece in ((0, coarse), (1, value - coarse)):
+                    row = (channel * 2 + part) * 128
+                    spread[row : row + 128, lanes] = jnp.where(
+                        here, jnp.broadcast_to(piece, (128, CAP)).astype(BF16), zero
+                    )
+            minor = jnp.broadcast_to(slots[5:6, :], (2 * LANES, CAP)).astype(BF16)
+            placed.append(jnp.where(minor == iota_minor, jnp.ones_like(minor), jnp.zeros_like(minor)))
+        summed = lax.dot_general(
+            spread[...], jnp.concatenate(placed, axis=1), NT, preferred_element_type=F32
+        )
+        if start == 0:
+            total[...] = summed
+        else:
+            total[...] += summed
     for channel in range(4):
         row = channel * 256
         for half in range(2):
             lanes = slice(half * LANES, (half + 1) * LANES)
-            summed = total[row : row + 128, lanes] + total[row + 128 : row + 256, lanes]
-            out[channel, :, half * ROWS : (half + 1) * ROWS, :] = summed.reshape(EDGE, ROWS, LANES)
+            both = total[row : row + 128, lanes] + total[row + 128 : row + 256, lanes]
+            out[channel, :, half * ROWS : (half + 1) * ROWS, :] = both.reshape(EDGE, ROWS, LANES)
 
 
 def lane_up(value):
@@ -286,6 +316,11 @@
 def row_down(value, before):
     row = lax.broadcasted_iota(jnp.int32, value.shape, 0)
     return jnp.where(row == 0, before, pltpu.roll(value, 1, 0))
+
+
+def has_neighbours():
+    line = lax.axis_index("gx")
+    return line > 0, line < lax.axis_size("gx") - 1
 
 
 M_LOW = 2 * HALO
@@ -310,11 +345,12 @@
             return upper[M_LOW + axis_no, :, :]
         return void[layer, :, :] * flow[axis_no, layer, :, :]
 
+    inside_left, inside_right = has_neighbours()
     for layer in range(EDGE):
         own = void[layer, :, :]
         row = (HALO + layer) * ROWS
-        void_left = left[row + ROWS - 1 : row + ROWS, :]
-        void_right = right[row : row + 1, :]
+        void_left = jnp.where(inside_left, left[row + ROWS - 1 : row + ROWS, :], 0.0)
+        void_right = jnp.where(inside_right, right[row : row + 1, :], 0.0)
         near = (
             void_layer(layer + 1), void_layer(layer - 1),
             row_up(own, void_right), row_down(own, void_left),
@@ -330,7 +366,8 @@
             row = M_ROWS + axis_no * EDGE + layer
             summed = (
                 moment_layer(axis_no, layer + 1) + moment_layer(axis_no, layer - 1)
-                + row_up(moment, right[row : row + 1, :]) + row_down(moment, left[row : row + 1, :])
+                + row_up(moment, jnp.where(inside_right, right[row : row + 1, :], 0.0))
+                + row_down(moment, jnp.where(inside_left, left[row : row + 1, :], 0.0))
                 + lane_up(moment) + lane_down(moment)
             )
             rate = VISCOSITY * (summed - mine * around) + (
@@ -404,11 +441,12 @@
 
 
 def widen_kernel(press, void, lower, upper, left, right, void_wide, press_wide, factor):
+    inside_left, inside_right = has_neighbours()
     for number, own, wide in ((0, void, void_wide), (1, press, press_wide)):
         for layer in range(WIDE):
             row = (number * WIDE + layer) * ROWS
-            wide[layer, 0:8, :] = left[row : row + ROWS, :]
-            wide[layer, 24:32, :] = right[row : row + ROWS, :]
+            wide[layer, 0:8, :] = jnp.where(inside_left, left[row : row + ROWS, :], 0.0)
+            wide[layer, 24:32, :] = jnp.where(inside_right, right[row : row + ROWS, :], 0.0)
             if layer < HALO:
                 wide[layer, 8:24, :] = lower[number * HALO + layer, :, :]
             elif layer < HALO + EDGE:
@@ -431,6 +469,7 @@
     trial, void_wide, press_wide, factor, wide_div, sent_left, sent_right, left, right,
     velocity_out, pressure_out, press, known, first, second,
 ):
+    inside_left, inside_right = has_neighbours()
     start = SPAN * ROWS
     for layer in range(SPAN):
         row = layer * ROWS
@@ -441,8 +480,8 @@
         block = jnp.concatenate([west, middle, east], axis=0)
         place = lax.broadcasted_iota(jnp.int32, (32, LANES), 0)
         block = block + jnp.where(place == 7, sent_left[edge, :], 0.0)
-        block = block - jnp.where(place == 8, left[edge, :], 0.0)
-        block = block + jnp.where(place == 23, right[edge, :], 0.0)
+        block = block - jnp.where((place == 8) & inside_left, left[edge, :], 0.0)
+        block = block + jnp.where((place == 23) & inside_right, right[edge, :], 0.0)
         block = block - jnp.where(place == 24, sent_right[edge, :], 0.0)
         known[layer + 1, :, :] = -2.0 * factor[layer + 1, :, :] * block
     for layer in range(WIDE):
@@ -485,16 +524,9 @@
             )
 
 
-def to_next(value, axis, periodic):
+def shifted(value, axis, steps):
     count = lax.axis_size(axis)
-    pairs = [(i, i + 1) for i in range(count - 1)] + ([(count - 1, 0)] if periodic else [])
-    return lax.ppermute(value, axis, pairs)
-
-
-def to_previous(value, axis, periodic):
-    count = lax.axis_size(axis)
-    pairs = [(i + 1, i) for i in range(count - 1)] + ([(0, count - 1)] if periodic else [])
-    return lax.ppermute(value, axis, pairs)
+    return lax.ppermute(value, axis, [(source, (source + steps) % count) for source in range(count)])
 
 
 def per_device(
@@ -504,58 +536,67 @@
     codes = remap_list.transpose(1, 2, 0).reshape(-1, remap_list.shape[0])
     fields = (velocity, history, pressure, void_fraction)
     bricks = (FIELDS * 32, LANES)
-    up, down = call(pack_kernel, [bricks, bricks], (codes,) + fields, smem=(0,))
-    brick_low = to_next(up, "gz", True)
-    brick_high = to_previous(down, "gz", True)
+    inputs = (codes,) + fields
+    up, down, code_of = call(
+        pack_kernel,
+        [bricks, bricks, jax.ShapeDtypeStruct((ROWS, LANES), jnp.int32)],
+        tuple(pltpu.with_memory_space_constraint(value, pltpu.HBM) for value in inputs),
+        spaces={number: pltpu.HBM for number in range(len(inputs))},
+        scratch=[(pltpu.SMEM if value is codes else pltpu.VMEM)(value.shape, value.dtype) for value in inputs]
+        + [pltpu.SemaphoreType.DMA((len(inputs),))],
+    )
     (outgoing,) = call(
         dispatch_kernel,
         [(OWNERS, 8, CAP)],
         (parcel_records, parcel_owner.reshape(32, 128), parcel_cells.reshape(32, 128)),
         scratch=(pltpu.VMEM((PARCELS // BLOCK * OWNERS, BLOCK), BF16), pltpu.VMEM((512, 2 * CAP), F32)),
     )
+    brick_low = shifted(up, "gz", 1)
+    brick_high = shifted(down, "gz", -1)
+    arrived = lax.all_to_all(outgoing, "gz", split_axis=0, concat_axis=0, tiled=True)
     layers = (2 * HALO + 3, EDGE, LANES)
-    flow, latest, base, press, void, up, down = call(
-        remap_kernel,
-        [(3,) + cells, (3,) + cells, (3,) + cells, cells, cells, layers, layers],
-        (codes,) + fields + (brick_low, brick_high),
-        smem=(0,),
-    )
-    state_low = to_next(up, "gz", True)
-    state_high = to_previous(down, "gz", True)
-    arrived = lax.all_to_all(outgoing, "gz", split_axis=0, concat_axis=0, tiled=True)
+    remap_inputs = (code_of,) + fields + (brick_low, brick_high)
+    press, void, up, down = call(remap_first_kernel, [cells, cells, layers, layers], remap_inputs)
+    state_low = shifted(up, "gz", 1)
+    state_high = shifted(down, "gz", -1)
+    flow, latest, base = call(remap_rest_kernel, [(3,) + cells] * 3, remap_inputs)
+    (deposit,) = call(
+        deposit_kernel,
+        [(4,) + cells],
+        (arrived,),
+        scratch=(pltpu.VMEM((1024, 2 * LANES), F32), pltpu.VMEM((1024, STEP * CAP), BF16)),
+    )
     rows = (2 * WIDE * ROWS + 3 * EDGE, LANES)
-    right, left = call(pack_rows_kernel, [rows, rows], (flow, press, void, state_low, state_high))
-    state_left = to_next(right, "gx", False)
-    state_right = to_previous(left, "gx", False)
-    (deposit,) = call(
-        deposit_kernel, [(4,) + cells], (arrived,), scratch=(pltpu.VMEM((1024, 2 * LANES), F32),)
-    )
-    layers = (REACH + 2, EDGE, LANES)
+    right, left = call(
+        pack_rows_kernel,
+        [rows, rows],
+        (flow, press, void, state_low, state_high),
+    )
+    state_left = shifted(right, "gx", 1)
+    state_right = shifted(left, "gx", -1)
     new_history, trial, div, up, down, edge = call(
         rate_kernel,
-        [(2, 3) + cells, (3,) + cells, cells, layers, layers, (2, EDGE, LANES)],
+        [(2, 3) + cells, (3,) + cells, cells, (REACH + 2,) + cells[1:], (REACH + 2,) + cells[1:], (2, EDGE, LANES)],
         (flow, latest, base, void, state_low, state_high, state_left, state_right, deposit),
         scratch=(pltpu.VMEM(cells, F32),),
     )
-    div_low = to_next(up, "gz", True)
-    div_high = to_previous(down, "gz", True)
-    wide = (WIDE, 32, LANES)
+    div_low = shifted(up, "gz", 1)
+    div_high = shifted(down, "gz", -1)
+    wide = (WIDE, 2 * EDGE, LANES)
     void_wide, press_wide, factor = call(
         widen_kernel, [wide, wide, wide], (press, void, state_low, state_high, state_left, state_right)
     )
     rows = (SPAN * ROWS + 32, LANES)
     wide_div, right, left = call(
-        pack_div_kernel,
-        [(SPAN, EDGE, LANES), rows, rows],
-        (div, down, up, edge, div_low, div_high),
-    )
-    div_left = to_next(right, "gx", False)
-    div_right = to_previous(left, "gx", False)
+        pack_div_kernel, [(SPAN, EDGE, LANES), rows, rows], (div, down, up, edge, div_low, div_high)
+    )
+    div_left = shifted(right, "gx", 1)
+    div_right = shifted(left, "gx", -1)
     new_velocity, new_pressure = call(
         relax_kernel,
         [(3,) + cells, cells],
         (trial, void_wide, press_wide, factor, wide_div, left, right, div_left, div_right),
-        scratch=(pltpu.VMEM(wide, F32), pltpu.VMEM(wide, F32), pltpu.VMEM(wide, F32), pltpu.VMEM(wide, F32)),
+        scratch=[pltpu.VMEM(wide, F32) for _ in range(4)],
     )
     return new_velocity, new_pressure, new_history
 

time: 87.7 us -> 69.9 us (0.80)
  starting transfers between devices: 45.2 us -> 36.8 us
  Pallas kernels: 25 us -> 18.9 us
  local copies, waits for them, and re-layouts: 4.68 us -> 0.04 us
  waiting for transfers between devices: 11.7 us -> 13.1 us
    ppermute x10, starting transfers between devices: 38.3 us -> 29.9 us  [shifted(): lax.ppermute(value, axis, [(source, (source + steps) % count) for source...]
    pallas_call x9 -> x10, Pallas kernels: 25 us -> 18.9 us  [call(): pl.pallas_call(kernel, out_shape=shapes, in_specs=[pl.BlockSpec(memory_sp...]
    unnamed x26 -> x18, local copies, waits for them, and re-layouts: 4.68 us -> 0.04 us
    ppermute x10, waiting for transfers between devices: 11.6 us -> 13.1 us  [shifted(): lax.ppermute(value, axis, [(source, (source + steps) % count) for source...]
  transfers between devices with their start and end apart: 11 -> 11, of which waited for: 3 -> 5; matrix products, arithmetic and copies ran while one was open for 0% -> 0% of each run, Pallas kernels for 22% -> 18%
where the time goes in v1:
time: 69.9 us; the launch traced here: 69.7 us
  starting transfers between devices  36.8 us (53%)
  Pallas kernels  18.9 us (27%)
  waiting for transfers between devices  13.1 us (19%)
  between operations  0.8 us (1%)
    ppermute x10, starting transfers between devices, shifted(): lax.ppermute(value, axis, [(source, (source + steps) % count) for source...  29.9 us
    pallas_call x10, Pallas kernels, call(): pl.pallas_call(kernel, out_shape=shapes, in_specs=[pl.BlockSpec(memory_sp...  18.9 us
    ppermute x10, waiting for transfers between devices, shifted(): lax.ppermute(value, axis, [(source, (source + steps) % count) for source...  13.1 us
    all_to_all x1, starting transfers between devices, per_device(): lax.all_to_all(outgoing, 'gz', split_axis=0, concat_axis=0, tiled=True)  6.9 us
  transfers between devices with their start and end apart: 11, of which 5 were waited for; matrix products, arithmetic and copies ran while one was open for 0% of the time, Pallas kernels for 18%

profile of v1, /device:TPU:1, one launch (start us, length us, event | category | flops | bytes accessed | tf_op | source)
XLA Modules:
  0.0 69.7 jit_solution(7215271168872121618)
XLA Ops:
  0.6 0.0 copy-start.6
  0.6 0.0 copy-start.7
  0.7 0.0 copy-start.8
  0.7 0.0 copy-start.1
  0.7 2.3 %shard_map.103 = (f32[352,128]{1,0:T(8,128)S(1)}, f32[352,128]{1,0:T(8,128)S(1)}, s32[8,128]{1,0:T(8,128)S(1)}) custom-call(s32[32,64]{1,0:T(8,128)} %bitcast.7, f32[3,16,16,128]{3,2,1,0:T(8,128)} %velocity.3, f32[2,3,16,16,128]{4,3,2,1,0:T(8,128)} %history.3, f32[16,16,128]{2,1,0:T(8,128)} %pressure.3, f32[16,16,128]{2,1,0:T(8,128)} %void.3), custom_call_target="tpu_custom_call" | custom-call | tf_op jit(solution)/shard_map/pallas_call | solution.py:41
  2.9 0.0 copy-start
  2.9 3.8 %collective-permute-start = (f32[352,128]{1,0:T(8,128)S(1)}, f32[352,128]{1,0:T(8,128)S(1)}, u32[]{:S(2)}, u32[]{:S(2)}) collective-permute-start(f32[352,128]{1,0:T(8,128)S(1)} %get-tuple-element.30), channel_id=1, source_target_pairs={{0,4},{4,8},{8,12},{12,16},{16,20},{20,24},{24,28},{28,32},{32,36}... | collective-permute-start | bytes 540680 | tf_op jit(solution)/shard_map/ppermute | solution.py:529
  6.8 7.6 %collective-permute-start.1 = (f32[352,128]{1,0:T(8,128)S(1)}, f32[352,128]{1,0:T(8,128)S(1)}, u32[]{:S(2)}, u32[]{:S(2)}) collective-permute-start(f32[352,128]{1,0:T(8,128)S(1)} %get-tuple-element.31), channel_id=1, source_target_pairs={{0,252},{4,0},{8,4},{12,8},{16,12},{20,16},{24,20},{28,24},{32,28}... | collective-permute-start | bytes 540680 | tf_op jit(solution)/shard_map/ppermute | solution.py:529
  14.3 0.0 copy-done.6
  14.3 0.0 copy-done.7
  14.3 0.0 copy-done.8
  14.4 2.8 %shard_map.107 = f32[64,8,128]{2,1,0:T(8,128)} custom-call(f32[16,4096]{1,0:T(8,128)S(1)} %copy-done.6, s32[32,128]{1,0:T(8,128)S(1)} %bitcast.5, s32[32,128]{1,0:T(8,128)S(1)} %bitcast.6), custom_call_target="tpu_custom_call" | custom-call | tf_op jit(solution)/shard_map/pallas_call | solution.py:41
  17.1 0.0 copy-start.2
  17.1 0.0 copy-start.3
  17.1 6.9 %all-to-all-start = ((f32[64,8,128]{2,1,0:T(8,128)}), f32[64,8,128]{2,1,0:T(8,128)S(1)}, u32[]{:S(2)}, u32[]{:S(2)}) async-start(f32[64,8,128]{2,1,0:T(8,128)} %shard_map.107), calls=%async_computation | async-start | bytes 524288 | tf_op jit(solution)/shard_map/all_to_all | solution.py:556
  24.0 0.0 collective-permute-done.lower
  24.0 0.0 collective-permute-done.1.upper
  24.0 0.0 copy-done.1
  24.1 0.0 copy-done
  24.1 0.0 copy-done.2
  24.1 0.0 copy-done.3
  24.1 0.6 shard_map.105
  24.7 2.6 %collective-permute-start.2 = (f32[17,16,128]{2,1,0:T(8,128)S(1)}, f32[17,16,128]{2,1,0:T(8,128)S(1)}, u32[]{:S(2)}, u32[]{:S(2)}) collective-permute-start(f32[17,16,128]{2,1,0:T(8,128)S(1)} %get-tuple-element.36), channel_id=1, source_target_pairs={{0,4},{4,8},{8,12},{12,16},{16,20},{20,24},{24,28},{28,32},{32,36}... | collective-permute-start | bytes 417800 | tf_op jit(solution)/shard_map/ppermute | solution.py:529
  27.3 4.7 %collective-permute-start.3 = (f32[17,16,128]{2,1,0:T(8,128)S(1)}, f32[17,16,128]{2,1,0:T(8,128)S(1)}, u32[]{:S(2)}, u32[]{:S(2)}) collective-permute-start(f32[17,16,128]{2,1,0:T(8,128)S(1)} %get-tuple-element.37), channel_id=1, source_target_pairs={{0,252},{4,0},{8,4},{12,8},{16,12},{20,16},{24,20},{28,24},{32,28}... | collective-permute-start | bytes 417800 | tf_op jit(solution)/shard_map/ppermute | solution.py:529
  31.9 1.8 %shard_map.104 = (f32[3,16,16,128]{3,2,1,0:T(8,128)S(1)}, f32[3,16,16,128]{3,2,1,0:T(8,128)S(1)}, f32[3,16,16,128]{3,2,1,0:T(8,128)S(1)}) custom-call(s32[8,128]{1,0:T(8,128)S(1)} %get-tuple-element.29.codes, f32[3,16,16,128]{3,2,1,0:T(8,128)S(1)} %copy-done.1, f32[2,3,16,16,128]{4,3,2,1,0:T(8,128)S(1)} %copy-done, f32[16,16,128]{2,1,0:T(8,128)S(1)} %copy-done.2, ...), custom_call_target="tpu_custom_call" | custom-call | tf_op jit(solution)/shard_map/pallas_call | solution.py:41
  33.8 0.0 copy-start.4
  33.8 5.3 %collective-permute-done.2.lower = f32[17,16,128]{2,1,0:T(8,128)S(1)} collective-permute-done((f32[17,16,128]{2,1,0:T(8,128)S(1)}, f32[17,16,128]{2,1,0:T(8,128)S(1)}, u32[]{:S(2)}, u32[]{:S(2)}) %collective-permute-start.2) | collective-permute-done | bytes 139296 | tf_op jit(solution)/shard_map/ppermute | solution.py:529
  39.0 0.0 collective-permute-done.3.upper
  39.0 0.8 %shard_map.106 = (f32[528,128]{1,0:T(8,128)}, f32[528,128]{1,0:T(8,128)S(1)}) custom-call(f32[3,16,16,128]{3,2,1,0:T(8,128)S(1)} %get-tuple-element.32.flow, f32[16,16,128]{2,1,0:T(8,128)S(1)} %get-tuple-element.38.press, f32[16,16,128]{2,1,0:T(8,128)S(1)} %get-tuple-element.35.void, f32[17,16,128]{2,1,0:T(8,128)S(1)} %collective-permute-done.2.lower, ...), custom_call_target="tpu_custom_call" | custom-call | tf_op jit(solution)/shard_map/pallas_call | solution.py:41
  39.8 0.0 copy-done.4
  39.8 2.7 %collective-permute-start.4 = (f32[528,128]{1,0:T(8,128)}, f32[528,128]{1,0:T(8,128)S(1)}, u32[]{:S(2)}, u32[]{:S(2)}) collective-permute-start(f32[528,128]{1,0:T(8,128)} %get-tuple-element.39), channel_id=1, source_target_pairs={{0,1},{1,2},{2,3},{3,0},{4,5},{5,6},{6,7},{7,4},{8,9},{9,10},{10,1... | collective-permute-start | bytes 811016 | tf_op jit(solution)/shard_map/ppermute | solution.py:529
  42.5 0.0 copy-start.5
  42.5 0.0 collective-permute-start.5
  42.5 0.0 all-to-all-done.arrived
  42.5 6.3 %shard_map.108.deposit = f32[4,16,16,128]{3,2,1,0:T(8,128)S(1)} custom-call(f32[64,8,128]{2,1,0:T(8,128)S(1)} %all-to-all-done.arrived), custom_call_target="tpu_custom_call" | custom-call | tf_op jit(solution)/shard_map/pallas_call | solution.py:41
  48.8 0.0 collective-permute-done.4.left
  48.8 1.3 %collective-permute-done.5.right = f32[528,128]{1,0:T(8,128)S(1)} collective-permute-done((f32[528,128]{1,0:T(8,128)S(1)}, f32[528,128]{1,0:T(8,128)S(1)}, u32[]{:S(2)}, u32[]{:S(2)}) %collective-permute-start.5) | collective-permute-done | bytes 270368 | tf_op jit(solution)/shard_map/ppermute | solution.py:529
  50.2 0.0 copy-done.5
  50.2 1.9 %shard_map.109 = (f32[2,3,16,16,128]{4,3,2,1,0:T(8,128)}, f32[3,16,16,128]{3,2,1,0:T(8,128)S(1)}, f32[16,16,128]{2,1,0:T(8,128)S(1)}, f32[8,16,128]{2,1,0:T(8,12...) custom-call(f32[3,16,16,128]{3,2,1,0:T(8,128)S(1)} %get-tuple-element.32.flow, ...), custom_call_target="tpu_custom_call" | custom-call | tf_op jit(solution)/shard_map/pallas_call | solution.py:41
  52.1 0.0 collective-permute-start.6
  52.1 7.2 %collective-permute-start.7 = (f32[8,16,128]{2,1,0:T(8,128)S(1)}, f32[8,16,128]{2,1,0:T(8,128)S(1)}, u32[]{:S(2)}, u32[]{:S(2)}) collective-permute-start(f32[8,16,128]{2,1,0:T(8,128)S(1)} %get-tuple-element.46.sent_lower), channel_id=1, source_target_pairs={{0,252},{4,0},{8,4},{12,8},{16,12},{20,16},{24,20},{28,24},{32,28}... | collective-permute-start | bytes 196616 | tf_op jit(solution)/shard_map/ppermute | solution.py:529
  59.3 2.4 %collective-permute-done.6.lower = f32[8,16,128]{2,1,0:T(8,128)S(1)} collective-permute-done((f32[8,16,128]{2,1,0:T(8,128)S(1)}, f32[8,16,128]{2,1,0:T(8,128)S(1)}, u32[]{:S(2)}, u32[]{:S(2)}) %collective-permute-start.6) | collective-permute-done | bytes 65568 | tf_op jit(solution)/shard_map/ppermute | solution.py:529
  61.7 0.0 collective-permute-done.7.upper
  61.8 1.4 %collective-permute-start.8 = (f32[256,128]{1,0:T(8,128)S(1)}, f32[256,128]{1,0:T(8,128)S(1)}, u32[]{:S(2)}, u32[]{:S(2)}) collective-permute-start(f32[256,128]{1,0:T(8,128)S(1)} %get-tuple-element.51.sent_right), channel_id=1, source_target_pairs={{0,1},{1,2},{2,3},{3,0},{4,5},{5,6},{6,7},{7,4},{8,9},{9,10},{10,1... | collective-permute-start | bytes 393224 | tf_op jit(solution)/shard_map/ppermute | solution.py:529
  63.1 0.0 collective-permute-start.9
  63.1 0.4 shard_map.110
  63.5 1.5 %collective-permute-done.8.left = f32[256,128]{1,0:T(8,128)S(1)} collective-permute-done((f32[256,128]{1,0:T(8,128)S(1)}, f32[256,128]{1,0:T(8,128)S(1)}, u32[]{:S(2)}, u32[]{:S(2)}) %collective-permute-start.8) | collective-permute-done | bytes 131104 | tf_op jit(solution)/shard_map/ppermute | solution.py:529
  65.1 2.5 %collective-permute-done.9.right = f32[256,128]{1,0:T(8,128)S(1)} collective-permute-done((f32[256,128]{1,0:T(8,128)S(1)}, f32[256,128]{1,0:T(8,128)S(1)}, u32[]{:S(2)}, u32[]{:S(2)}) %collective-permute-start.9) | collective-permute-done | bytes 131104 | tf_op jit(solution)/shard_map/ppermute | solution.py:529
  67.6 2.1 %shard_map.112 = (f32[3,16,16,128]{3,2,1,0:T(8,128)}, f32[16,16,128]{2,1,0:T(8,128)}) custom-call(f32[3,16,16,128]{3,2,1,0:T(8,128)S(1)} %get-tuple-element.41.trial, f32[30,32,128]{2,1,0:T(8,128)S(1)} %get-tuple-element.42.void_wide, f32[30,32,128]{2,1,0:T(8,128)S(1)} %get-tuple-element.43.press_wide, f32[30,32,128]{2,1,0:T(8,128)S(1)} %get-tuple-element.44.factor, ...), custom_call_target="tpu_custom_call" | custom-call | tf_op jit(solution)/shard_map/pallas_call | solution.py:41
  (1 shorter events, 0.0 us)
Async XLA Ops:
  0.6 13.7 %copy-start.6 = (f32[16,4096]{1,0:T(8,128)S(1)}, f32[16,4096]{1,0:T(8,128)}, u32[]{:S(2)}) copy-start(f32[16,4096]{1,0:T(8,128)} %records.1) | copy-start | bytes 786436
  0.6 13.7 %copy-start.7 = (s32[4096,1]{0,1:T(1,128)S(1)}, s32[4096,1]{0,1:T(1,128)}, u32[]{:S(2)}) copy-start(s32[4096,1]{0,1:T(1,128)} %param.14) | copy-start | bytes 49156
  0.7 13.7 %copy-start.8 = (s32[4096]{0:T(1024)S(1)}, s32[4096]{0:T(1024)}, u32[]{:S(2)}) copy-start(s32[4096]{0:T(1024)} %param.15) | copy-start | bytes 49156
  0.7 23.4 %copy-start.1 = (f32[3,16,16,128]{3,2,1,0:T(8,128)S(1)}, f32[3,16,16,128]{3,2,1,0:T(8,128)}, u32[]{:S(2)}) copy-start(f32[3,16,16,128]{3,2,1,0:T(8,128)} %velocity.3) | copy-start | bytes 1179652
  2.9 21.1 %copy-start = (f32[2,3,16,16,128]{4,3,2,1,0:T(8,128)S(1)}, f32[2,3,16,16,128]{4,3,2,1,0:T(8,128)}, u32[]{:S(2)}) copy-start(f32[2,3,16,16,128]{4,3,2,1,0:T(8,128)} %history.3) | copy-start | bytes 2359300
  2.9 21.1 %collective-permute-start = (f32[352,128]{1,0:T(8,128)S(1)}, f32[352,128]{1,0:T(8,128)S(1)}, u32[]{:S(2)}, u32[]{:S(2)}) collective-permute-start(f32[352,128]{1,0:T(8,128)S(1)} %get-tuple-element.30), channel_id=1, source_target_pairs={{0,4},{4,8},{8,12},{12,16},{16,20},{20,24},{24,28},{28,32},{32,36}... | collective-permute-start | bytes 540680 | tf_op jit(solution)/shard_map/ppermute | solution.py:529
  6.8 17.3 %collective-permute-start.1 = (f32[352,128]{1,0:T(8,128)S(1)}, f32[352,128]{1,0:T(8,128)S(1)}, u32[]{:S(2)}, u32[]{:S(2)}) collective-permute-start(f32[352,128]{1,0:T(8,128)S(1)} %get-tuple-element.31), channel_id=1, source_target_pairs={{0,252},{4,0},{8,4},{12,8},{16,12},{20,16},{24,20},{28,24},{32,28}... | collective-permute-start | bytes 540680 | tf_op jit(solution)/shard_map/ppermute | solution.py:529
  17.1 7.0 %copy-start.2 = (f32[16,16,128]{2,1,0:T(8,128)S(1)}, f32[16,16,128]{2,1,0:T(8,128)}, u32[]{:S(2)}) copy-start(f32[16,16,128]{2,1,0:T(8,128)} %pressure.3) | copy-start | bytes 393220
  17.1 7.0 %copy-start.3 = (f32[16,16,128]{2,1,0:T(8,128)S(1)}, f32[16,16,128]{2,1,0:T(8,128)}, u32[]{:S(2)}) copy-start(f32[16,16,128]{2,1,0:T(8,128)} %void.3) | copy-start | bytes 393220
  17.1 25.4 %all-to-all-start = ((f32[64,8,128]{2,1,0:T(8,128)}), f32[64,8,128]{2,1,0:T(8,128)S(1)}, u32[]{:S(2)}, u32[]{:S(2)}) async-start(f32[64,8,128]{2,1,0:T(8,128)} %shard_map.107), calls=%async_computation | async-start | bytes 524288 | tf_op jit(solution)/shard_map/all_to_all | solution.py:556
  24.7 14.3 %collective-permute-start.2 = (f32[17,16,128]{2,1,0:T(8,128)S(1)}, f32[17,16,128]{2,1,0:T(8,128)S(1)}, u32[]{:S(2)}, u32[]{:S(2)}) collective-permute-start(f32[17,16,128]{2,1,0:T(8,128)S(1)} %get-tuple-element.36), channel_id=1, source_target_pairs={{0,4},{4,8},{8,12},{12,16},{16,20},{20,24},{24,28},{28,32},{32,36}... | collective-permute-start | bytes 417800 | tf_op jit(solution)/shard_map/ppermute | solution.py:529
  27.3 11.8 %collective-permute-start.3 = (f32[17,16,128]{2,1,0:T(8,128)S(1)}, f32[17,16,128]{2,1,0:T(8,128)S(1)}, u32[]{:S(2)}, u32[]{:S(2)}) collective-permute-start(f32[17,16,128]{2,1,0:T(8,128)S(1)} %get-tuple-element.37), channel_id=1, source_target_pairs={{0,252},{4,0},{8,4},{12,8},{16,12},{20,16},{24,20},{28,24},{32,28}... | collective-permute-start | bytes 417800 | tf_op jit(solution)/shard_map/ppermute | solution.py:529
  33.8 6.1 %copy-start.4 = (f32[3,16,16,128]{3,2,1,0:T(8,128)}, f32[3,16,16,128]{3,2,1,0:T(8,128)S(1)}, u32[]{:S(2)}) copy-start(f32[3,16,16,128]{3,2,1,0:T(8,128)S(1)} %get-tuple-element.34.base) | copy-start | bytes 1179652
  39.8 9.0 %collective-permute-start.4 = (f32[528,128]{1,0:T(8,128)}, f32[528,128]{1,0:T(8,128)S(1)}, u32[]{:S(2)}, u32[]{:S(2)}) collective-permute-start(f32[528,128]{1,0:T(8,128)} %get-tuple-element.39), channel_id=1, source_target_pairs={{0,1},{1,2},{2,3},{3,0},{4,5},{5,6},{6,7},{7,4},{8,9},{9,10},{10,1... | collective-permute-start | bytes 811016 | tf_op jit(solution)/shard_map/ppermute | solution.py:529
  42.5 7.6 %copy-start.5 = (f32[3,16,16,128]{3,2,1,0:T(8,128)S(1)}, f32[3,16,16,128]{3,2,1,0:T(8,128)}, u32[]{:S(2)}) copy-start(f32[3,16,16,128]{3,2,1,0:T(8,128)} %copy-done.4) | copy-start | bytes 1179652
  42.5 7.6 %collective-permute-start.5 = (f32[528,128]{1,0:T(8,128)S(1)}, f32[528,128]{1,0:T(8,128)S(1)}, u32[]{:S(2)}, u32[]{:S(2)}) collective-permute-start(f32[528,128]{1,0:T(8,128)S(1)} %get-tuple-element.40), channel_id=1, source_target_pairs={{0,3},{1,0},{2,1},{3,2},{4,7},{5,4},{6,5},{7,6},{8,11},{9,8},{10,9... | collective-permute-start | bytes 811016 | tf_op jit(solution)/shard_map/ppermute | solution.py:529
  52.1 9.6 %collective-permute-start.6 = (f32[8,16,128]{2,1,0:T(8,128)S(1)}, f32[8,16,128]{2,1,0:T(8,128)S(1)}, u32[]{:S(2)}, u32[]{:S(2)}) collective-permute-start(f32[8,16,128]{2,1,0:T(8,128)S(1)} %get-tuple-element.47.sent_upper), channel_id=1, source_target_pairs={{0,4},{4,8},{8,12},{12,16},{16,20},{20,24},{24,28},{28,32},{32,36}... | collective-permute-start | bytes 196616 | tf_op jit(solution)/shard_map/ppermute | solution.py:529
  52.1 9.6 %collective-permute-start.7 = (f32[8,16,128]{2,1,0:T(8,128)S(1)}, f32[8,16,128]{2,1,0:T(8,128)S(1)}, u32[]{:S(2)}, u32[]{:S(2)}) collective-permute-start(f32[8,16,128]{2,1,0:T(8,128)S(1)} %get-tuple-element.46.sent_lower), channel_id=1, source_target_pairs={{0,252},{4,0},{8,4},{12,8},{16,12},{20,16},{24,20},{28,24},{32,28}... | collective-permute-start | bytes 196616 | tf_op jit(solution)/shard_map/ppermute | solution.py:529
  61.8 3.3 %collective-permute-start.8 = (f32[256,128]{1,0:T(8,128)S(1)}, f32[256,128]{1,0:T(8,128)S(1)}, u32[]{:S(2)}, u32[]{:S(2)}) collective-permute-start(f32[256,128]{1,0:T(8,128)S(1)} %get-tuple-element.51.sent_right), channel_id=1, source_target_pairs={{0,1},{1,2},{2,3},{3,0},{4,5},{5,6},{6,7},{7,4},{8,9},{9,10},{10,1... | collective-permute-start | bytes 393224 | tf_op jit(solution)/shard_map/ppermute | solution.py:529
  63.1 4.4 %collective-permute-start.9 = (f32[256,128]{1,0:T(8,128)S(1)}, f32[256,128]{1,0:T(8,128)S(1)}, u32[]{:S(2)}, u32[]{:S(2)}) collective-permute-start(f32[256,128]{1,0:T(8,128)S(1)} %get-tuple-element.50.sent_left), channel_id=1, source_target_pairs={{0,3},{1,0},{2,1},{3,2},{4,7},{5,4},{6,5},{7,6},{8,11},{9,8},{10,9... | collective-permute-start | bytes 393224 | tf_op jit(solution)/shard_map/ppermute | solution.py:529

commit v2 on v1

--- a/solution.py
+++ b/solution.py
@@ -29,22 +29,28 @@
 PARCELS = 4096
 BLOCK = 256
 STEP = 4
-VMEM_LIMIT = 48 * 1024 * 1024
+VMEM_LIMIT = 16 * 1024 * 1024
 
 F32 = jnp.float32
 BF16 = jnp.bfloat16
 
 
-def call(kernel, outs, args, spaces=None, scratch=()):
+def call(kernel, outs, args, spaces=None, scratch=(), far=(), aliases=None):
     spaces = spaces or {}
     shapes = [out if isinstance(out, jax.ShapeDtypeStruct) else jax.ShapeDtypeStruct(out, F32) for out in outs]
+    shapes = [
+        pltpu.HBM(shape.shape, shape.dtype) if number in far else shape for number, shape in enumerate(shapes)
+    ]
     return pl.pallas_call(
         kernel,
         out_shape=shapes,
         in_specs=[
             pl.BlockSpec(memory_space=spaces.get(number, pltpu.VMEM)) for number in range(len(args))
         ],
-        out_specs=[pl.BlockSpec(memory_space=pltpu.VMEM) for _ in outs],
+        out_specs=[
+            pl.BlockSpec(memory_space=pltpu.HBM if number in far else pltpu.VMEM) for number in range(len(outs))
+        ],
+        input_output_aliases=aliases or {},
         scratch_shapes=list(scratch),
         compiler_params=pltpu.CompilerParams(vmem_limit_bytes=VMEM_LIMIT),
     )(*args)
@@ -69,7 +75,7 @@
     return (pressure if field == 9 else void)[layer, rows, :]
 
 
-def pack_bricks(codes, refs, to_upper, to_lower, code_out):
+def pack_bricks(codes, refs, to_upper, to_lower, code_out, arrive):
     cycle = lax.axis_index("gz")
     line = lax.axis_index("gx")
     size = lax.axis_size("gz")
@@ -89,7 +95,8 @@
     code_out[...] = code_of
     index_up = slot_up * BRICK + lane % BRICK
     index_down = slot_down * BRICK + lane % BRICK
-    for field in range(FIELDS):
+    for field in (10, 9, 0, 1, 2, 3, 4, 5, 6, 7, 8):
+        arrive(field)
         for part in range(4):
             up = jnp.zeros((ROWS, LANES), F32)
             down = jnp.zeros((ROWS, LANES), F32)
@@ -112,11 +119,16 @@
 def pack_kernel(*refs):
     sources, (to_upper, to_lower, code_out), held, arrivals = refs[:5], refs[5:8], refs[8:13], refs[13]
     copies = copied(sources, held, arrivals)
-    for copy in copies:
-        copy.start()
-    for copy in copies:
-        copy.wait()
-    pack_bricks(held[0], held[1:], to_upper, to_lower, code_out)
+    for number in (0, 4, 3, 1, 2):
+        copies[number].start()
+    copies[0].wait()
+
+    def arrive(field):
+        number = {10: 4, 9: 3, 0: 1, 3: 2}.get(field)
+        if number is not None:
+            copies[number].wait()
+
+    pack_bricks(held[0], held[1:], to_upper, to_lower, code_out, arrive)
 
 
 def remapper(code_ref, refs, lower, upper):
@@ -165,9 +177,11 @@
 
 
 def remap_rest_kernel(
-    codes, velocity, history, pressure, void, lower, upper, flow_out, latest_out, base_out
+    codes, velocity, history, pressure, void, lower, upper, flow_out, base_far, latest_far,
+    base_out, latest_out, leaving,
 ):
     moved = remapper(codes, (velocity, history, pressure, void), lower, upper)
+    copies = []
     for tile in range(32):
         layer, rows = tile_at(tile)
         for axis_no in range(3):
@@ -177,6 +191,15 @@
             base_out[axis_no, layer, rows, :] = flow + TIME_STEP * (
                 WEIGHT_OLDER * older - WEIGHT_LAST * latest
             )
+        if tile % 8 == 7:
+            part = pl.ds(tile // 8 * 4, 4)
+            for source, target in ((base_out, base_far), (latest_out, latest_far)):
+                copies.append(
+                    pltpu.make_async_copy(source.at[:, part], target.at[:, part], leaving.at[len(copies)])
+                )
+                copies[-1].start()
+    for copy in copies:
+        copy.wait()
 
 
 def pack_rows_kernel(flow, press, void, lower, upper, to_right, to_left):
@@ -262,11 +285,11 @@
         out[owner, :, :] = total[row : row + 8, lanes] + total[row + 8 : row + 16, lanes]
 
 
-def deposit_kernel(arrived, out, total, spread):
+def add_slots(arrived, sources, total, spread):
     iota_major = lax.broadcasted_iota(jnp.int32, (128, CAP), 0).astype(F32).astype(BF16)
     iota_minor = lax.broadcasted_iota(jnp.int32, (2 * LANES, CAP), 0).astype(F32).astype(BF16)
     zero = jnp.zeros((128, CAP), BF16)
-    for start in range(0, OWNERS, STEP):
+    for start in sources:
         placed = []
         for place in range(STEP):
             slots = arrived[start + place, :, :]
@@ -289,6 +312,10 @@
             total[...] = summed
         else:
             total[...] += summed
+
+
+def deposit_kernel(arrived, out, total, spread):
+    add_slots(arrived, range(0, OWNERS, STEP), total, spread)
     for channel in range(4):
         row = channel * 256
         for half in range(2):
@@ -329,8 +356,10 @@
 
 def rate_kernel(
     flow, latest, base, void, lower, upper, left, right, deposit,
-    history_out, trial_out, div_out, to_upper, to_lower, edge_out, scaled,
+    history_out, trial_out, div_out, to_upper, to_lower, edge_out, scaled, arrival,
 ):
+    last = pltpu.make_async_copy(latest, history_out.at[1], arrival)
+    last.start()
     def void_layer(layer):
         if layer < 0:
             return lower[HALO + layer, :, :]
@@ -374,7 +403,6 @@
                 deposit[axis_no, layer, :, :] - drag * mine
             ) * inverse
             history_out[0, axis_no, layer, :, :] = rate
-            history_out[1, axis_no, layer, :, :] = latest[axis_no, layer, :, :]
             trial = base[axis_no, layer, :, :] + (TIME_STEP * WEIGHT_NEW) * rate
             trial_out[axis_no, layer, :, :] = trial
             part = trial * (near[2 * axis_no] - near[2 * axis_no + 1])
@@ -405,6 +433,7 @@
         for side in range(2):
             send[REACH + 1, side * 8 : side * 8 + REACH, :] = edge_out[side, start : start + REACH, :]
             send[REACH + 1, side * 8 + REACH : side * 8 + 8, :] = jnp.zeros((8 - REACH, LANES), F32)
+    last.wait()
 
 
 def pack_div_kernel(div, sent_lower, sent_upper, edge, lower, upper, wide_out, to_right, to_left):
@@ -559,26 +588,33 @@
     press, void, up, down = call(remap_first_kernel, [cells, cells, layers, layers], remap_inputs)
     state_low = shifted(up, "gz", 1)
     state_high = shifted(down, "gz", -1)
-    flow, latest, base = call(remap_rest_kernel, [(3,) + cells] * 3, remap_inputs)
-    (deposit,) = call(
-        deposit_kernel,
-        [(4,) + cells],
-        (arrived,),
-        scratch=(pltpu.VMEM((1024, 2 * LANES), F32), pltpu.VMEM((1024, STEP * CAP), BF16)),
-    )
+    flow, base, latest = call(
+        remap_rest_kernel,
+        [(3,) + cells] * 3,
+        remap_inputs,
+        scratch=[pltpu.VMEM((3,) + cells, F32)] * 2 + [pltpu.SemaphoreType.DMA((8,))],
+        far=(1, 2),
+    )
+    sums = (1024, 2 * LANES)
+    spread = pltpu.VMEM((1024, STEP * CAP), BF16)
     rows = (2 * WIDE * ROWS + 3 * EDGE, LANES)
     right, left = call(
         pack_rows_kernel,
         [rows, rows],
         (flow, press, void, state_low, state_high),
     )
+    (deposit,) = call(
+        deposit_kernel, [(4,) + cells], (arrived,), scratch=(pltpu.VMEM(sums, F32), spread)
+    )
     state_left = shifted(right, "gx", 1)
     state_right = shifted(left, "gx", -1)
+    latest = pltpu.with_memory_space_constraint(latest, pltpu.HBM)
     new_history, trial, div, up, down, edge = call(
         rate_kernel,
         [(2, 3) + cells, (3,) + cells, cells, (REACH + 2,) + cells[1:], (REACH + 2,) + cells[1:], (2, EDGE, LANES)],
         (flow, latest, base, void, state_low, state_high, state_left, state_right, deposit),
-        scratch=(pltpu.VMEM(cells, F32),),
+        spaces={1: pltpu.HBM},
+        scratch=(pltpu.VMEM(cells, F32), pltpu.SemaphoreType.DMA(())),
     )
     div_low = shifted(up, "gz", 1)
     div_high = shifted(down, "gz", -1)

time: 69.9 us -> 69.1 us (0.989)
  waiting for transfers between devices: 13.1 us -> 12 us
    ppermute x10, waiting for transfers between devices: 13.1 us -> 12 us  [shifted(): lax.ppermute(value, axis, [(source, (source + steps) % count) for source...]
where the time goes in v2:
time: 69.1 us; the launch traced here: 68.9 us
  starting transfers between devices  37.1 us (54%)
  Pallas kernels  19 us (27%)
  waiting for transfers between devices  12 us (17%)
  between operations  0.81 us (1%)
    ppermute x10, starting transfers between devices, shifted(): lax.ppermute(value, axis, [(source, (source + steps) % count) for source...  30.2 us
    pallas_call x10, Pallas kernels, call(): pl.pallas_call(kernel, out_shape=shapes, in_specs=[pl.BlockSpec(memory_sp...  19 us
    ppermute x10, waiting for transfers between devices, shifted(): lax.ppermute(value, axis, [(source, (source + steps) % count) for source...  12 us
    all_to_all x1, starting transfers between devices, per_device(): lax.all_to_all(outgoing, 'gz', split_axis=0, concat_axis=0, tiled=True)  6.9 us
  transfers between devices with their start and end apart: 11, of which 5 were waited for; matrix products, arithmetic and copies ran while one was open for 0% of the time, Pallas kernels for 18%

profile of v2, /device:TPU:1, one launch (start us, length us, event | category | flops | bytes accessed | tf_op | source)
XLA Modules:
  0.0 68.9 jit_solution(10436952058817821358)
XLA Ops:
  0.6 0.0 copy-start.5
  0.6 0.0 copy-start.6
  0.7 0.0 copy-start.7
  0.7 0.0 copy-start.1
  0.7 2.2 %shard_map.103 = (f32[352,128]{1,0:T(8,128)S(1)}, f32[352,128]{1,0:T(8,128)S(1)}, s32[8,128]{1,0:T(8,128)S(1)}) custom-call(s32[32,64]{1,0:T(8,128)} %bitcast.7, f32[3,16,16,128]{3,2,1,0:T(8,128)} %velocity.3, f32[2,3,16,16,128]{4,3,2,1,0:T(8,128)} %history.3, f32[16,16,128]{2,1,0:T(8,128)} %pressure.3, f32[16,16,128]{2,1,0:T(8,128)} %void.3), custom_call_target="tpu_custom_call" | custom-call | tf_op jit(solution)/shard_map/pallas_call | solution.py:44
  2.9 0.0 copy-start
  2.9 3.8 %collective-permute-start = (f32[352,128]{1,0:T(8,128)S(1)}, f32[352,128]{1,0:T(8,128)S(1)}, u32[]{:S(2)}, u32[]{:S(2)}) collective-permute-start(f32[352,128]{1,0:T(8,128)S(1)} %get-tuple-element.30), channel_id=1, source_target_pairs={{0,4},{4,8},{8,12},{12,16},{16,20},{20,24},{24,28},{28,32},{32,36}... | collective-permute-start | bytes 540680 | tf_op jit(solution)/shard_map/ppermute | solution.py:558
  6.7 7.6 %collective-permute-start.1 = (f32[352,128]{1,0:T(8,128)S(1)}, f32[352,128]{1,0:T(8,128)S(1)}, u32[]{:S(2)}, u32[]{:S(2)}) collective-permute-start(f32[352,128]{1,0:T(8,128)S(1)} %get-tuple-element.31), channel_id=1, source_target_pairs={{0,252},{4,0},{8,4},{12,8},{16,12},{20,16},{24,20},{28,24},{32,28}... | collective-permute-start | bytes 540680 | tf_op jit(solution)/shard_map/ppermute | solution.py:558
  14.3 0.0 copy-done.5
  14.3 0.0 copy-done.6
  14.3 0.0 copy-done.7
  14.3 2.8 %shard_map.107 = f32[64,8,128]{2,1,0:T(8,128)} custom-call(f32[16,4096]{1,0:T(8,128)S(1)} %copy-done.5, s32[32,128]{1,0:T(8,128)S(1)} %bitcast.5, s32[32,128]{1,0:T(8,128)S(1)} %bitcast.6), custom_call_target="tpu_custom_call" | custom-call | tf_op jit(solution)/shard_map/pallas_call | solution.py:44
  17.1 0.0 copy-start.2
  17.1 0.0 copy-start.3
  17.1 6.9 %all-to-all-start = ((f32[64,8,128]{2,1,0:T(8,128)}), f32[64,8,128]{2,1,0:T(8,128)S(1)}, u32[]{:S(2)}, u32[]{:S(2)}) async-start(f32[64,8,128]{2,1,0:T(8,128)} %shard_map.107), calls=%async_computation | async-start | bytes 524288 | tf_op jit(solution)/shard_map/all_to_all | solution.py:585
  24.0 0.0 collective-permute-done.lower
  24.0 0.0 collective-permute-done.1.upper
  24.0 0.0 copy-done.1
  24.0 0.0 copy-done
  24.0 0.0 copy-done.2
  24.0 0.0 copy-done.3
  24.0 0.6 shard_map.105
  24.6 2.6 %collective-permute-start.2 = (f32[17,16,128]{2,1,0:T(8,128)S(1)}, f32[17,16,128]{2,1,0:T(8,128)S(1)}, u32[]{:S(2)}, u32[]{:S(2)}) collective-permute-start(f32[17,16,128]{2,1,0:T(8,128)S(1)} %get-tuple-element.36), channel_id=1, source_target_pairs={{0,4},{4,8},{8,12},{12,16},{16,20},{20,24},{24,28},{28,32},{32,36}... | collective-permute-start | bytes 417800 | tf_op jit(solution)/shard_map/ppermute | solution.py:558
  27.2 4.7 %collective-permute-start.3 = (f32[17,16,128]{2,1,0:T(8,128)S(1)}, f32[17,16,128]{2,1,0:T(8,128)S(1)}, u32[]{:S(2)}, u32[]{:S(2)}) collective-permute-start(f32[17,16,128]{2,1,0:T(8,128)S(1)} %get-tuple-element.37), channel_id=1, source_target_pairs={{0,252},{4,0},{8,4},{12,8},{16,12},{20,16},{24,20},{28,24},{32,28}... | collective-permute-start | bytes 417800 | tf_op jit(solution)/shard_map/ppermute | solution.py:558
  31.9 2.6 %shard_map.104 = (f32[3,16,16,128]{3,2,1,0:T(8,128)S(1)}, f32[3,16,16,128]{3,2,1,0:T(8,128)}, f32[3,16,16,128]{3,2,1,0:T(8,128)}) custom-call(s32[8,128]{1,0:T(8,128)S(1)} %get-tuple-element.29.codes, f32[3,16,16,128]{3,2,1,0:T(8,128)S(1)} %copy-done.1, f32[2,3,16,16,128]{4,3,2,1,0:T(8,128)S(1)} %copy-done, f32[16,16,128]{2,1,0:T(8,128)S(1)} %copy-done.2, ...), custom_call_target="tpu_custom_call" | custom-call | tf_op jit(solution)/shard_map/pallas_call | solution.py:44
  34.4 4.5 %collective-permute-done.2.lower = f32[17,16,128]{2,1,0:T(8,128)S(1)} collective-permute-done((f32[17,16,128]{2,1,0:T(8,128)S(1)}, f32[17,16,128]{2,1,0:T(8,128)S(1)}, u32[]{:S(2)}, u32[]{:S(2)}) %collective-permute-start.2) | collective-permute-done | bytes 139296 | tf_op jit(solution)/shard_map/ppermute | solution.py:558
  39.0 0.0 collective-permute-done.3.upper
  39.0 0.1 shard_map.106
  39.0 2.8 %collective-permute-start.4 = (f32[528,128]{1,0:T(8,128)S(1)}, f32[528,128]{1,0:T(8,128)S(1)}, u32[]{:S(2)}, u32[]{:S(2)}) collective-permute-start(f32[528,128]{1,0:T(8,128)S(1)} %get-tuple-element.39), channel_id=1, source_target_pairs={{0,1},{1,2},{2,3},{3,0},{4,5},{5,6},{6,7},{7,4},{8,9},{9,10},{10,1... | collective-permute-start | bytes 811016 | tf_op jit(solution)/shard_map/ppermute | solution.py:558
  41.8 0.0 copy-start.4
  41.8 0.0 collective-permute-start.5
  41.8 0.0 all-to-all-done.arrived
  41.8 6.3 %shard_map.108.deposit = f32[4,16,16,128]{3,2,1,0:T(8,128)S(1)} custom-call(f32[64,8,128]{2,1,0:T(8,128)S(1)} %all-to-all-done.arrived), custom_call_target="tpu_custom_call" | custom-call | tf_op jit(solution)/shard_map/pallas_call | solution.py:44
  48.1 0.0 collective-permute-done.4.left
  48.1 1.1 %collective-permute-done.5.right = f32[528,128]{1,0:T(8,128)S(1)} collective-permute-done((f32[528,128]{1,0:T(8,128)S(1)}, f32[528,128]{1,0:T(8,128)S(1)}, u32[]{:S(2)}, u32[]{:S(2)}) %collective-permute-start.5) | collective-permute-done | bytes 270368 | tf_op jit(solution)/shard_map/ppermute | solution.py:558
  49.3 0.0 copy-done.4
  49.3 2.0 %shard_map.109 = (f32[2,3,16,16,128]{4,3,2,1,0:T(8,128)}, f32[3,16,16,128]{3,2,1,0:T(8,128)S(1)}, f32[16,16,128]{2,1,0:T(8,128)S(1)}, f32[8,16,128]{2,1,0:T(8,12...) custom-call(f32[3,16,16,128]{3,2,1,0:T(8,128)S(1)} %get-tuple-element.32.flow, ...), custom_call_target="tpu_custom_call" | custom-call | tf_op jit(solution)/shard_map/pallas_call | solution.py:44
  51.3 0.1 collective-permute-start.6
  51.3 7.2 %collective-permute-start.7 = (f32[8,16,128]{2,1,0:T(8,128)S(1)}, f32[8,16,128]{2,1,0:T(8,128)S(1)}, u32[]{:S(2)}, u32[]{:S(2)}) collective-permute-start(f32[8,16,128]{2,1,0:T(8,128)S(1)} %get-tuple-element.46.sent_lower), channel_id=1, source_target_pairs={{0,252},{4,0},{8,4},{12,8},{16,12},{20,16},{24,20},{28,24},{32,28}... | collective-permute-start | bytes 196616 | tf_op jit(solution)/shard_map/ppermute | solution.py:558
  58.5 2.3 %collective-permute-done.6.lower = f32[8,16,128]{2,1,0:T(8,128)S(1)} collective-permute-done((f32[8,16,128]{2,1,0:T(8,128)S(1)}, f32[8,16,128]{2,1,0:T(8,128)S(1)}, u32[]{:S(2)}, u32[]{:S(2)}) %collective-permute-start.6) | collective-permute-done | bytes 65568 | tf_op jit(solution)/shard_map/ppermute | solution.py:558
  60.8 0.0 collective-permute-done.7.upper
  60.9 1.5 %collective-permute-start.8 = (f32[256,128]{1,0:T(8,128)S(1)}, f32[256,128]{1,0:T(8,128)S(1)}, u32[]{:S(2)}, u32[]{:S(2)}) collective-permute-start(f32[256,128]{1,0:T(8,128)S(1)} %get-tuple-element.51.sent_right), channel_id=1, source_target_pairs={{0,1},{1,2},{2,3},{3,0},{4,5},{5,6},{6,7},{7,4},{8,9},{9,10},{10,1... | collective-permute-start | bytes 393224 | tf_op jit(solution)/shard_map/ppermute | solution.py:558
  62.3 0.0 collective-permute-start.9
  62.4 0.4 shard_map.110
  62.8 1.5 %collective-permute-done.8.left = f32[256,128]{1,0:T(8,128)S(1)} collective-permute-done((f32[256,128]{1,0:T(8,128)S(1)}, f32[256,128]{1,0:T(8,128)S(1)}, u32[]{:S(2)}, u32[]{:S(2)}) %collective-permute-start.8) | collective-permute-done | bytes 131104 | tf_op jit(solution)/shard_map/ppermute | solution.py:558
  64.3 2.5 %collective-permute-done.9.right = f32[256,128]{1,0:T(8,128)S(1)} collective-permute-done((f32[256,128]{1,0:T(8,128)S(1)}, f32[256,128]{1,0:T(8,128)S(1)}, u32[]{:S(2)}, u32[]{:S(2)}) %collective-permute-start.9) | collective-permute-done | bytes 131104 | tf_op jit(solution)/shard_map/ppermute | solution.py:558
  66.8 2.1 %shard_map.112 = (f32[3,16,16,128]{3,2,1,0:T(8,128)}, f32[16,16,128]{2,1,0:T(8,128)}) custom-call(f32[3,16,16,128]{3,2,1,0:T(8,128)S(1)} %get-tuple-element.41.trial, f32[30,32,128]{2,1,0:T(8,128)S(1)} %get-tuple-element.42.void_wide, f32[30,32,128]{2,1,0:T(8,128)S(1)} %get-tuple-element.43.press_wide, f32[30,32,128]{2,1,0:T(8,128)S(1)} %get-tuple-element.44.factor, ...), custom_call_target="tpu_custom_call" | custom-call | tf_op jit(solution)/shard_map/pallas_call | solution.py:44
  (1 shorter events, 0.0 us)
Async XLA Ops:
  0.6 13.7 %copy-start.5 = (f32[16,4096]{1,0:T(8,128)S(1)}, f32[16,4096]{1,0:T(8,128)}, u32[]{:S(2)}) copy-start(f32[16,4096]{1,0:T(8,128)} %records.1) | copy-start | bytes 786436
  0.6 13.7 %copy-start.6 = (s32[4096,1]{0,1:T(1,128)S(1)}, s32[4096,1]{0,1:T(1,128)}, u32[]{:S(2)}) copy-start(s32[4096,1]{0,1:T(1,128)} %param.14) | copy-start | bytes 49156
  0.7 13.6 %copy-start.7 = (s32[4096]{0:T(1024)S(1)}, s32[4096]{0:T(1024)}, u32[]{:S(2)}) copy-start(s32[4096]{0:T(1024)} %param.15) | copy-start | bytes 49156
  0.7 23.3 %copy-start.1 = (f32[3,16,16,128]{3,2,1,0:T(8,128)S(1)}, f32[3,16,16,128]{3,2,1,0:T(8,128)}, u32[]{:S(2)}) copy-start(f32[3,16,16,128]{3,2,1,0:T(8,128)} %velocity.3) | copy-start | bytes 1179652
  2.9 21.1 %copy-start = (f32[2,3,16,16,128]{4,3,2,1,0:T(8,128)S(1)}, f32[2,3,16,16,128]{4,3,2,1,0:T(8,128)}, u32[]{:S(2)}) copy-start(f32[2,3,16,16,128]{4,3,2,1,0:T(8,128)} %history.3) | copy-start | bytes 2359300
  2.9 21.1 %collective-permute-start = (f32[352,128]{1,0:T(8,128)S(1)}, f32[352,128]{1,0:T(8,128)S(1)}, u32[]{:S(2)}, u32[]{:S(2)}) collective-permute-start(f32[352,128]{1,0:T(8,128)S(1)} %get-tuple-element.30), channel_id=1, source_target_pairs={{0,4},{4,8},{8,12},{12,16},{16,20},{20,24},{24,28},{28,32},{32,36}... | collective-permute-start | bytes 540680 | tf_op jit(solution)/shard_map/ppermute | solution.py:558
  6.7 17.3 %collective-permute-start.1 = (f32[352,128]{1,0:T(8,128)S(1)}, f32[352,128]{1,0:T(8,128)S(1)}, u32[]{:S(2)}, u32[]{:S(2)}) collective-permute-start(f32[352,128]{1,0:T(8,128)S(1)} %get-tuple-element.31), channel_id=1, source_target_pairs={{0,252},{4,0},{8,4},{12,8},{16,12},{20,16},{24,20},{28,24},{32,28}... | collective-permute-start | bytes 540680 | tf_op jit(solution)/shard_map/ppermute | solution.py:558
  17.1 7.0 %copy-start.2 = (f32[16,16,128]{2,1,0:T(8,128)S(1)}, f32[16,16,128]{2,1,0:T(8,128)}, u32[]{:S(2)}) copy-start(f32[16,16,128]{2,1,0:T(8,128)} %pressure.3) | copy-start | bytes 393220
  17.1 7.0 %copy-start.3 = (f32[16,16,128]{2,1,0:T(8,128)S(1)}, f32[16,16,128]{2,1,0:T(8,128)}, u32[]{:S(2)}) copy-start(f32[16,16,128]{2,1,0:T(8,128)} %void.3) | copy-start | bytes 393220
  17.1 24.8 %all-to-all-start = ((f32[64,8,128]{2,1,0:T(8,128)}), f32[64,8,128]{2,1,0:T(8,128)S(1)}, u32[]{:S(2)}, u32[]{:S(2)}) async-start(f32[64,8,128]{2,1,0:T(8,128)} %shard_map.107), calls=%async_computation | async-start | bytes 524288 | tf_op jit(solution)/shard_map/all_to_all | solution.py:585
  24.6 14.3 %collective-permute-start.2 = (f32[17,16,128]{2,1,0:T(8,128)S(1)}, f32[17,16,128]{2,1,0:T(8,128)S(1)}, u32[]{:S(2)}, u32[]{:S(2)}) collective-permute-start(f32[17,16,128]{2,1,0:T(8,128)S(1)} %get-tuple-element.36), channel_id=1, source_target_pairs={{0,4},{4,8},{8,12},{12,16},{16,20},{20,24},{24,28},{28,32},{32,36}... | collective-permute-start | bytes 417800 | tf_op jit(solution)/shard_map/ppermute | solution.py:558
  27.2 11.8 %collective-permute-start.3 = (f32[17,16,128]{2,1,0:T(8,128)S(1)}, f32[17,16,128]{2,1,0:T(8,128)S(1)}, u32[]{:S(2)}, u32[]{:S(2)}) collective-permute-start(f32[17,16,128]{2,1,0:T(8,128)S(1)} %get-tuple-element.37), channel_id=1, source_target_pairs={{0,252},{4,0},{8,4},{12,8},{16,12},{20,16},{24,20},{28,24},{32,28}... | collective-permute-start | bytes 417800 | tf_op jit(solution)/shard_map/ppermute | solution.py:558
  39.0 9.1 %collective-permute-start.4 = (f32[528,128]{1,0:T(8,128)S(1)}, f32[528,128]{1,0:T(8,128)S(1)}, u32[]{:S(2)}, u32[]{:S(2)}) collective-permute-start(f32[528,128]{1,0:T(8,128)S(1)} %get-tuple-element.39), channel_id=1, source_target_pairs={{0,1},{1,2},{2,3},{3,0},{4,5},{5,6},{6,7},{7,4},{8,9},{9,10},{10,1... | collective-permute-start | bytes 811016 | tf_op jit(solution)/shard_map/ppermute | solution.py:558
  41.8 7.4 %copy-start.4 = (f32[3,16,16,128]{3,2,1,0:T(8,128)S(1)}, f32[3,16,16,128]{3,2,1,0:T(8,128)}, u32[]{:S(2)}) copy-start(f32[3,16,16,128]{3,2,1,0:T(8,128)} %get-tuple-element.34.base) | copy-start | bytes 1179652
  41.8 7.4 %collective-permute-start.5 = (f32[528,128]{1,0:T(8,128)S(1)}, f32[528,128]{1,0:T(8,128)S(1)}, u32[]{:S(2)}, u32[]{:S(2)}) collective-permute-start(f32[528,128]{1,0:T(8,128)S(1)} %get-tuple-element.40), channel_id=1, source_target_pairs={{0,3},{1,0},{2,1},{3,2},{4,7},{5,4},{6,5},{7,6},{8,11},{9,8},{10,9... | collective-permute-start | bytes 811016 | tf_op jit(solution)/shard_map/ppermute | solution.py:558
  51.3 9.6 %collective-permute-start.6 = (f32[8,16,128]{2,1,0:T(8,128)S(1)}, f32[8,16,128]{2,1,0:T(8,128)S(1)}, u32[]{:S(2)}, u32[]{:S(2)}) collective-permute-start(f32[8,16,128]{2,1,0:T(8,128)S(1)} %get-tuple-element.47.sent_upper), channel_id=1, source_target_pairs={{0,4},{4,8},{8,12},{12,16},{16,20},{20,24},{24,28},{28,32},{32,36}... | collective-permute-start | bytes 196616 | tf_op jit(solution)/shard_map/ppermute | solution.py:558
  51.3 9.5 %collective-permute-start.7 = (f32[8,16,128]{2,1,0:T(8,128)S(1)}, f32[8,16,128]{2,1,0:T(8,128)S(1)}, u32[]{:S(2)}, u32[]{:S(2)}) collective-permute-start(f32[8,16,128]{2,1,0:T(8,128)S(1)} %get-tuple-element.46.sent_lower), channel_id=1, source_target_pairs={{0,252},{4,0},{8,4},{12,8},{16,12},{20,16},{24,20},{28,24},{32,28}... | collective-permute-start | bytes 196616 | tf_op jit(solution)/shard_map/ppermute | solution.py:558
  60.9 3.4 %collective-permute-start.8 = (f32[256,128]{1,0:T(8,128)S(1)}, f32[256,128]{1,0:T(8,128)S(1)}, u32[]{:S(2)}, u32[]{:S(2)}) collective-permute-start(f32[256,128]{1,0:T(8,128)S(1)} %get-tuple-element.51.sent_right), channel_id=1, source_target_pairs={{0,1},{1,2},{2,3},{3,0},{4,5},{5,6},{6,7},{7,4},{8,9},{9,10},{10,1... | collective-permute-start | bytes 393224 | tf_op jit(solution)/shard_map/ppermute | solution.py:558
  62.3 4.4 %collective-permute-start.9 = (f32[256,128]{1,0:T(8,128)S(1)}, f32[256,128]{1,0:T(8,128)S(1)}, u32[]{:S(2)}, u32[]{:S(2)}) collective-permute-start(f32[256,128]{1,0:T(8,128)S(1)} %get-tuple-element.50.sent_left), channel_id=1, source_target_pairs={{0,3},{1,0},{2,1},{3,2},{4,7},{5,4},{6,5},{7,6},{8,11},{9,8},{10,9... | collective-permute-start | bytes 393224 | tf_op jit(solution)/shard_map/ppermute | solution.py:558

commit v3 on v2

--- a/solution.py
+++ b/solution.py
@@ -229,25 +229,28 @@
 
 def dispatch_kernel(records, owners, cells, out, shown, total):
     blocks = PARCELS // BLOCK
-    owner_iota = lax.broadcasted_iota(jnp.int32, (OWNERS, BLOCK), 0)
+    owner_iota = lax.broadcasted_iota(jnp.int32, (OWNERS, BLOCK), 0).astype(F32).astype(BF16)
     before = (
         lax.broadcasted_iota(jnp.int32, (BLOCK, BLOCK), 0)
         < lax.broadcasted_iota(jnp.int32, (BLOCK, BLOCK), 1)
     ).astype(F32).astype(BF16)
 
+    one, none = jnp.ones((2 * CAP, BLOCK), BF16), jnp.zeros((2 * CAP, BLOCK), BF16)
+
     def row_of(ref, block):
         return jnp.concatenate([ref[2 * block : 2 * block + 1, :], ref[2 * block + 1 : 2 * block + 2, :]], axis=1)
 
     for block in range(blocks):
-        hit = (row_of(owners, block) == owner_iota).astype(F32)
-        shown[block * OWNERS : (block + 1) * OWNERS, :] = hit.astype(BF16)
+        named = jnp.broadcast_to(row_of(owners, block).astype(F32), (OWNERS, BLOCK)).astype(BF16)
+        shown[block * OWNERS : (block + 1) * OWNERS, :] = jnp.where(
+            named == owner_iota, one[0:OWNERS, :], none[0:OWNERS, :]
+        )
     earlier = lax.dot_general(
         shown[...], before, (((1,), (0,)), ((), ())), preferred_element_type=F32
     )
     base = jnp.zeros((OWNERS, 1), F32)
     row_iota = lax.broadcasted_iota(jnp.int32, (4, BLOCK), 0)
-    key_iota = lax.broadcasted_iota(jnp.int32, (2 * CAP, BLOCK), 0)
-    total[...] = jnp.zeros_like(total)
+    key_iota = lax.broadcasted_iota(jnp.int32, (2 * CAP, BLOCK), 0).astype(F32).astype(BF16)
     for block in range(blocks):
         rows = slice(block * OWNERS, (block + 1) * OWNERS)
         hit = shown[rows, :].astype(F32)
@@ -257,7 +260,9 @@
         owner = row_of(owners, block)
         cell = row_of(cells, block)
         key = (owner // 32) * CAP + rank
-        placed = (key == key_iota).astype(F32).astype(BF16)
+        placed = jnp.where(
+            jnp.broadcast_to(key.astype(F32), (2 * CAP, BLOCK)).astype(BF16) == key_iota, one, none
+        )
         lanes = slice(block * BLOCK, (block + 1) * BLOCK)
         terms = jnp.zeros((4, BLOCK), F32)
         for size_class in range(4):
@@ -278,7 +283,11 @@
             [jnp.where(group == jnp.asarray(number, BF16), values, jnp.zeros_like(values)) for number in range(32)],
             axis=0,
         )
-        total[...] += lax.dot_general(spread, placed, NT, preferred_element_type=F32)
+        summed = lax.dot_general(spread, placed, NT, preferred_element_type=F32)
+        if block == 0:
+            total[...] = summed
+        else:
+            total[...] += summed
     for owner in range(OWNERS):
         row = (owner % 32) * 16
         lanes = slice((owner // 32) * CAP, (owner // 32 + 1) * CAP)
@@ -356,10 +365,10 @@
 
 def rate_kernel(
     flow, latest, base, void, lower, upper, left, right, deposit,
-    history_out, trial_out, div_out, to_upper, to_lower, edge_out, scaled, arrival,
+    history_out, trial_out, div_out, to_upper, to_lower, edge_out, scaled, rates, leaving,
 ):
-    last = pltpu.make_async_copy(latest, history_out.at[1], arrival)
-    last.start()
+    copies = [pltpu.make_async_copy(latest, history_out.at[1], leaving.at[0])]
+    copies[0].start()
     def void_layer(layer):
         if layer < 0:
             return lower[HALO + layer, :, :]
@@ -402,7 +411,7 @@
             rate = VISCOSITY * (summed - mine * around) + (
                 deposit[axis_no, layer, :, :] - drag * mine
             ) * inverse
-            history_out[0, axis_no, layer, :, :] = rate
+            rates[axis_no, layer, :, :] = rate
             trial = base[axis_no, layer, :, :] + (TIME_STEP * WEIGHT_NEW) * rate
             trial_out[axis_no, layer, :, :] = trial
             part = trial * (near[2 * axis_no] - near[2 * axis_no + 1])
@@ -417,6 +426,14 @@
             if axis_no == 2:
                 slope = slope + lane_up(weighted) - lane_down(weighted)
         div_out[layer, :, :] = slope
+        if layer % 4 == 3:
+            part = pl.ds(layer - 3, 4)
+            copies.append(
+                pltpu.make_async_copy(
+                    rates.at[:, part], history_out.at[0].at[:, part], leaving.at[len(copies)]
+                )
+            )
+            copies[-1].start()
     for layer in range(EDGE):
         total = div_out[layer, :, :]
         if layer < EDGE - 1:
@@ -433,7 +450,8 @@
         for side in range(2):
             send[REACH + 1, side * 8 : side * 8 + REACH, :] = edge_out[side, start : start + REACH, :]
             send[REACH + 1, side * 8 + REACH : side * 8 + 8, :] = jnp.zeros((8 - REACH, LANES), F32)
-    last.wait()
+    for copy in copies:
+        copy.wait()
 
 
 def pack_div_kernel(div, sent_lower, sent_upper, edge, lower, upper, wide_out, to_right, to_left):
@@ -614,7 +632,8 @@
         [(2, 3) + cells, (3,) + cells, cells, (REACH + 2,) + cells[1:], (REACH + 2,) + cells[1:], (2, EDGE, LANES)],
         (flow, latest, base, void, state_low, state_high, state_left, state_right, deposit),
         spaces={1: pltpu.HBM},
-        scratch=(pltpu.VMEM(cells, F32), pltpu.SemaphoreType.DMA(())),
+        scratch=(pltpu.VMEM(cells, F32), pltpu.VMEM((3,) + cells, F32), pltpu.SemaphoreType.DMA((5,))),
+        far=(0,),
     )
     div_low = shifted(up, "gz", 1)
     div_high = shifted(down, "gz", -1)

time: 69.1 us -> 80.1 us (1.16)
  Pallas kernels: 19 us -> 29.9 us
    pallas_call x10, Pallas kernels: 19 us -> 29.9 us  [call(): pl.pallas_call(kernel, out_shape=shapes, in_specs=[pl.BlockSpec(memory_sp...]
  transfers between devices with their start and end apart: 11 -> 11, of which waited for: 5 -> 5; matrix products, arithmetic and copies ran while one was open for 0% -> 0% of each run, Pallas kernels for 18% -> 16%
where the time goes in v3:
time: 80.1 us; the launch traced here: 79.9 us
  starting transfers between devices  37.1 us (46%)
  Pallas kernels  29.9 us (37%)
  waiting for transfers between devices  12 us (15%)
  between operations  0.81 us (1%)
    ppermute x10, starting transfers between devices, shifted(): lax.ppermute(value, axis, [(source, (source + steps) % count) for source...  30.2 us
    pallas_call x10, Pallas kernels, call(): pl.pallas_call(kernel, out_shape=shapes, in_specs=[pl.BlockSpec(memory_sp...  29.9 us
    ppermute x10, waiting for transfers between devices, shifted(): lax.ppermute(value, axis, [(source, (source + steps) % count) for source...  12 us
    all_to_all x1, starting transfers between devices, per_device(): lax.all_to_all(outgoing, 'gz', split_axis=0, concat_axis=0, tiled=True)  6.9 us
  transfers between devices with their start and end apart: 11, of which 5 were waited for; matrix products, arithmetic and copies ran while one was open for 0% of the time, Pallas kernels for 16%

profile of v3, /device:TPU:1, one launch (start us, length us, event | category | flops | bytes accessed | tf_op | source)
XLA Modules:
  0.0 79.9 jit_solution(15260604554056723845)
XLA Ops:
  0.6 0.0 copy-start.5
  0.6 0.0 copy-start.6
  0.7 0.0 copy-start.7
  0.7 0.0 copy-start.1
  0.7 2.2 %shard_map.103 = (f32[352,128]{1,0:T(8,128)S(1)}, f32[352,128]{1,0:T(8,128)S(1)}, s32[8,128]{1,0:T(8,128)S(1)}) custom-call(s32[32,64]{1,0:T(8,128)} %bitcast.7, f32[3,16,16,128]{3,2,1,0:T(8,128)} %velocity.3, f32[2,3,16,16,128]{4,3,2,1,0:T(8,128)} %history.3, f32[16,16,128]{2,1,0:T(8,128)} %pressure.3, f32[16,16,128]{2,1,0:T(8,128)} %void.3), custom_call_target="tpu_custom_call" | custom-call | tf_op jit(solution)/shard_map/pallas_call | solution.py:44
  2.9 0.0 copy-start
  2.9 3.8 %collective-permute-start = (f32[352,128]{1,0:T(8,128)S(1)}, f32[352,128]{1,0:T(8,128)S(1)}, u32[]{:S(2)}, u32[]{:S(2)}) collective-permute-start(f32[352,128]{1,0:T(8,128)S(1)} %get-tuple-element.30), channel_id=1, source_target_pairs={{0,4},{4,8},{8,12},{12,16},{16,20},{20,24},{24,28},{28,32},{32,36}... | collective-permute-start | bytes 540680 | tf_op jit(solution)/shard_map/ppermute | solution.py:576
  6.7 7.6 %collective-permute-start.1 = (f32[352,128]{1,0:T(8,128)S(1)}, f32[352,128]{1,0:T(8,128)S(1)}, u32[]{:S(2)}, u32[]{:S(2)}) collective-permute-start(f32[352,128]{1,0:T(8,128)S(1)} %get-tuple-element.31), channel_id=1, source_target_pairs={{0,252},{4,0},{8,4},{12,8},{16,12},{20,16},{24,20},{28,24},{32,28}... | collective-permute-start | bytes 540680 | tf_op jit(solution)/shard_map/ppermute | solution.py:576
  14.3 0.0 copy-done.5
  14.3 0.0 copy-done.6
  14.3 0.0 copy-done.7
  14.3 2.6 %shard_map.107 = f32[64,8,128]{2,1,0:T(8,128)} custom-call(f32[16,4096]{1,0:T(8,128)S(1)} %copy-done.5, s32[32,128]{1,0:T(8,128)S(1)} %bitcast.5, s32[32,128]{1,0:T(8,128)S(1)} %bitcast.6), custom_call_target="tpu_custom_call" | custom-call | tf_op jit(solution)/shard_map/pallas_call | solution.py:44
  16.9 0.0 copy-start.2
  16.9 0.0 copy-start.3
  16.9 6.9 %all-to-all-start = ((f32[64,8,128]{2,1,0:T(8,128)}), f32[64,8,128]{2,1,0:T(8,128)S(1)}, u32[]{:S(2)}, u32[]{:S(2)}) async-start(f32[64,8,128]{2,1,0:T(8,128)} %shard_map.107), calls=%async_computation | async-start | bytes 524288 | tf_op jit(solution)/shard_map/all_to_all | solution.py:603
  23.9 0.0 collective-permute-done.lower
  23.9 0.0 collective-permute-done.1.upper
  23.9 0.0 copy-done.1
  23.9 0.0 copy-done
  23.9 0.0 copy-done.2
  23.9 0.0 copy-done.3
  23.9 0.6 shard_map.105
  24.5 2.6 %collective-permute-start.2 = (f32[17,16,128]{2,1,0:T(8,128)S(1)}, f32[17,16,128]{2,1,0:T(8,128)S(1)}, u32[]{:S(2)}, u32[]{:S(2)}) collective-permute-start(f32[17,16,128]{2,1,0:T(8,128)S(1)} %get-tuple-element.36), channel_id=1, source_target_pairs={{0,4},{4,8},{8,12},{12,16},{16,20},{20,24},{24,28},{28,32},{32,36}... | collective-permute-start | bytes 417800 | tf_op jit(solution)/shard_map/ppermute | solution.py:576
  27.1 4.7 %collective-permute-start.3 = (f32[17,16,128]{2,1,0:T(8,128)S(1)}, f32[17,16,128]{2,1,0:T(8,128)S(1)}, u32[]{:S(2)}, u32[]{:S(2)}) collective-permute-start(f32[17,16,128]{2,1,0:T(8,128)S(1)} %get-tuple-element.37), channel_id=1, source_target_pairs={{0,252},{4,0},{8,4},{12,8},{16,12},{20,16},{24,20},{28,24},{32,28}... | collective-permute-start | bytes 417800 | tf_op jit(solution)/shard_map/ppermute | solution.py:576
  31.8 2.6 %shard_map.104 = (f32[3,16,16,128]{3,2,1,0:T(8,128)S(1)}, f32[3,16,16,128]{3,2,1,0:T(8,128)}, f32[3,16,16,128]{3,2,1,0:T(8,128)}) custom-call(s32[8,128]{1,0:T(8,128)S(1)} %get-tuple-element.29.codes, f32[3,16,16,128]{3,2,1,0:T(8,128)S(1)} %copy-done.1, f32[2,3,16,16,128]{4,3,2,1,0:T(8,128)S(1)} %copy-done, f32[16,16,128]{2,1,0:T(8,128)S(1)} %copy-done.2, ...), custom_call_target="tpu_custom_call" | custom-call | tf_op jit(solution)/shard_map/pallas_call | solution.py:44
  34.3 4.5 %collective-permute-done.2.lower = f32[17,16,128]{2,1,0:T(8,128)S(1)} collective-permute-done((f32[17,16,128]{2,1,0:T(8,128)S(1)}, f32[17,16,128]{2,1,0:T(8,128)S(1)}, u32[]{:S(2)}, u32[]{:S(2)}) %collective-permute-start.2) | collective-permute-done | bytes 139296 | tf_op jit(solution)/shard_map/ppermute | solution.py:576
  38.9 0.0 collective-permute-done.3.upper
  38.9 0.1 shard_map.106
  38.9 2.8 %collective-permute-start.4 = (f32[528,128]{1,0:T(8,128)S(1)}, f32[528,128]{1,0:T(8,128)S(1)}, u32[]{:S(2)}, u32[]{:S(2)}) collective-permute-start(f32[528,128]{1,0:T(8,128)S(1)} %get-tuple-element.39), channel_id=1, source_target_pairs={{0,1},{1,2},{2,3},{3,0},{4,5},{5,6},{6,7},{7,4},{8,9},{9,10},{10,1... | collective-permute-start | bytes 811016 | tf_op jit(solution)/shard_map/ppermute | solution.py:576
  41.7 0.0 copy-start.4
  41.7 0.0 collective-permute-start.5
  41.7 0.0 all-to-all-done.arrived
  41.7 6.3 %shard_map.108.deposit = f32[4,16,16,128]{3,2,1,0:T(8,128)S(1)} custom-call(f32[64,8,128]{2,1,0:T(8,128)S(1)} %all-to-all-done.arrived), custom_call_target="tpu_custom_call" | custom-call | tf_op jit(solution)/shard_map/pallas_call | solution.py:44
  48.0 0.0 collective-permute-done.4.left
  48.0 1.1 %collective-permute-done.5.right = f32[528,128]{1,0:T(8,128)S(1)} collective-permute-done((f32[528,128]{1,0:T(8,128)S(1)}, f32[528,128]{1,0:T(8,128)S(1)}, u32[]{:S(2)}, u32[]{:S(2)}) %collective-permute-start.5) | collective-permute-done | bytes 270368 | tf_op jit(solution)/shard_map/ppermute | solution.py:576
  49.2 0.0 copy-done.4
  49.2 13.1 %shard_map.109 = (f32[2,3,16,16,128]{4,3,2,1,0:T(8,128)}, f32[3,16,16,128]{3,2,1,0:T(8,128)S(1)}, f32[16,16,128]{2,1,0:T(8,128)S(1)}, f32[8,16,128]{2,1,0:T(8,12...) custom-call(f32[3,16,16,128]{3,2,1,0:T(8,128)S(1)} %get-tuple-element.32.flow, ...), custom_call_target="tpu_custom_call" | custom-call | tf_op jit(solution)/shard_map/pallas_call | solution.py:44
  62.2 0.1 collective-permute-start.6
  62.3 7.2 %collective-permute-start.7 = (f32[8,16,128]{2,1,0:T(8,128)S(1)}, f32[8,16,128]{2,1,0:T(8,128)S(1)}, u32[]{:S(2)}, u32[]{:S(2)}) collective-permute-start(f32[8,16,128]{2,1,0:T(8,128)S(1)} %get-tuple-element.46.sent_lower), channel_id=1, source_target_pairs={{0,252},{4,0},{8,4},{12,8},{16,12},{20,16},{24,20},{28,24},{32,28}... | collective-permute-start | bytes 196616 | tf_op jit(solution)/shard_map/ppermute | solution.py:576
  69.5 2.3 %collective-permute-done.6.lower = f32[8,16,128]{2,1,0:T(8,128)S(1)} collective-permute-done((f32[8,16,128]{2,1,0:T(8,128)S(1)}, f32[8,16,128]{2,1,0:T(8,128)S(1)}, u32[]{:S(2)}, u32[]{:S(2)}) %collective-permute-start.6) | collective-permute-done | bytes 65568 | tf_op jit(solution)/shard_map/ppermute | solution.py:576
  71.8 0.0 collective-permute-done.7.upper
  71.8 1.5 %collective-permute-start.8 = (f32[256,128]{1,0:T(8,128)S(1)}, f32[256,128]{1,0:T(8,128)S(1)}, u32[]{:S(2)}, u32[]{:S(2)}) collective-permute-start(f32[256,128]{1,0:T(8,128)S(1)} %get-tuple-element.51.sent_right), channel_id=1, source_target_pairs={{0,1},{1,2},{2,3},{3,0},{4,5},{5,6},{6,7},{7,4},{8,9},{9,10},{10,1... | collective-permute-start | bytes 393224 | tf_op jit(solution)/shard_map/ppermute | solution.py:576
  73.3 0.0 collective-permute-start.9
  73.3 0.4 shard_map.110
  73.7 1.5 %collective-permute-done.8.left = f32[256,128]{1,0:T(8,128)S(1)} collective-permute-done((f32[256,128]{1,0:T(8,128)S(1)}, f32[256,128]{1,0:T(8,128)S(1)}, u32[]{:S(2)}, u32[]{:S(2)}) %collective-permute-start.8) | collective-permute-done | bytes 131104 | tf_op jit(solution)/shard_map/ppermute | solution.py:576
  75.3 2.5 %collective-permute-done.9.right = f32[256,128]{1,0:T(8,128)S(1)} collective-permute-done((f32[256,128]{1,0:T(8,128)S(1)}, f32[256,128]{1,0:T(8,128)S(1)}, u32[]{:S(2)}, u32[]{:S(2)}) %collective-permute-start.9) | collective-permute-done | bytes 131104 | tf_op jit(solution)/shard_map/ppermute | solution.py:576
  77.8 2.1 %shard_map.112 = (f32[3,16,16,128]{3,2,1,0:T(8,128)}, f32[16,16,128]{2,1,0:T(8,128)}) custom-call(f32[3,16,16,128]{3,2,1,0:T(8,128)S(1)} %get-tuple-element.41.trial, f32[30,32,128]{2,1,0:T(8,128)S(1)} %get-tuple-element.42.void_wide, f32[30,32,128]{2,1,0:T(8,128)S(1)} %get-tuple-element.43.press_wide, f32[30,32,128]{2,1,0:T(8,128)S(1)} %get-tuple-element.44.factor, ...), custom_call_target="tpu_custom_call" | custom-call | tf_op jit(solution)/shard_map/pallas_call | solution.py:44
  (1 shorter events, 0.0 us)
Async XLA Ops:
  0.6 13.7 %copy-start.5 = (f32[16,4096]{1,0:T(8,128)S(1)}, f32[16,4096]{1,0:T(8,128)}, u32[]{:S(2)}) copy-start(f32[16,4096]{1,0:T(8,128)} %records.1) | copy-start | bytes 786436
  0.6 13.7 %copy-start.6 = (s32[4096,1]{0,1:T(1,128)S(1)}, s32[4096,1]{0,1:T(1,128)}, u32[]{:S(2)}) copy-start(s32[4096,1]{0,1:T(1,128)} %param.14) | copy-start | bytes 49156
  0.7 13.6 %copy-start.7 = (s32[4096]{0:T(1024)S(1)}, s32[4096]{0:T(1024)}, u32[]{:S(2)}) copy-start(s32[4096]{0:T(1024)} %param.15) | copy-start | bytes 49156
  0.7 23.2 %copy-start.1 = (f32[3,16,16,128]{3,2,1,0:T(8,128)S(1)}, f32[3,16,16,128]{3,2,1,0:T(8,128)}, u32[]{:S(2)}) copy-start(f32[3,16,16,128]{3,2,1,0:T(8,128)} %velocity.3) | copy-start | bytes 1179652
  2.9 21.0 %copy-start = (f32[2,3,16,16,128]{4,3,2,1,0:T(8,128)S(1)}, f32[2,3,16,16,128]{4,3,2,1,0:T(8,128)}, u32[]{:S(2)}) copy-start(f32[2,3,16,16,128]{4,3,2,1,0:T(8,128)} %history.3) | copy-start | bytes 2359300
  2.9 21.0 %collective-permute-start = (f32[352,128]{1,0:T(8,128)S(1)}, f32[352,128]{1,0:T(8,128)S(1)}, u32[]{:S(2)}, u32[]{:S(2)}) collective-permute-start(f32[352,128]{1,0:T(8,128)S(1)} %get-tuple-element.30), channel_id=1, source_target_pairs={{0,4},{4,8},{8,12},{12,16},{16,20},{20,24},{24,28},{28,32},{32,36}... | collective-permute-start | bytes 540680 | tf_op jit(solution)/shard_map/ppermute | solution.py:576
  6.7 17.2 %collective-permute-start.1 = (f32[352,128]{1,0:T(8,128)S(1)}, f32[352,128]{1,0:T(8,128)S(1)}, u32[]{:S(2)}, u32[]{:S(2)}) collective-permute-start(f32[352,128]{1,0:T(8,128)S(1)} %get-tuple-element.31), channel_id=1, source_target_pairs={{0,252},{4,0},{8,4},{12,8},{16,12},{20,16},{24,20},{28,24},{32,28}... | collective-permute-start | bytes 540680 | tf_op jit(solution)/shard_map/ppermute | solution.py:576
  16.9 7.0 %copy-start.2 = (f32[16,16,128]{2,1,0:T(8,128)S(1)}, f32[16,16,128]{2,1,0:T(8,128)}, u32[]{:S(2)}) copy-start(f32[16,16,128]{2,1,0:T(8,128)} %pressure.3) | copy-start | bytes 393220
  16.9 7.0 %copy-start.3 = (f32[16,16,128]{2,1,0:T(8,128)S(1)}, f32[16,16,128]{2,1,0:T(8,128)}, u32[]{:S(2)}) copy-start(f32[16,16,128]{2,1,0:T(8,128)} %void.3) | copy-start | bytes 393220
  16.9 24.8 %all-to-all-start = ((f32[64,8,128]{2,1,0:T(8,128)}), f32[64,8,128]{2,1,0:T(8,128)S(1)}, u32[]{:S(2)}, u32[]{:S(2)}) async-start(f32[64,8,128]{2,1,0:T(8,128)} %shard_map.107), calls=%async_computation | async-start | bytes 524288 | tf_op jit(solution)/shard_map/all_to_all | solution.py:603
  24.5 14.3 %collective-permute-start.2 = (f32[17,16,128]{2,1,0:T(8,128)S(1)}, f32[17,16,128]{2,1,0:T(8,128)S(1)}, u32[]{:S(2)}, u32[]{:S(2)}) collective-permute-start(f32[17,16,128]{2,1,0:T(8,128)S(1)} %get-tuple-element.36), channel_id=1, source_target_pairs={{0,4},{4,8},{8,12},{12,16},{16,20},{20,24},{24,28},{28,32},{32,36}... | collective-permute-start | bytes 417800 | tf_op jit(solution)/shard_map/ppermute | solution.py:576
  27.1 11.8 %collective-permute-start.3 = (f32[17,16,128]{2,1,0:T(8,128)S(1)}, f32[17,16,128]{2,1,0:T(8,128)S(1)}, u32[]{:S(2)}, u32[]{:S(2)}) collective-permute-start(f32[17,16,128]{2,1,0:T(8,128)S(1)} %get-tuple-element.37), channel_id=1, source_target_pairs={{0,252},{4,0},{8,4},{12,8},{16,12},{20,16},{24,20},{28,24},{32,28}... | collective-permute-start | bytes 417800 | tf_op jit(solution)/shard_map/ppermute | solution.py:576
  38.9 9.1 %collective-permute-start.4 = (f32[528,128]{1,0:T(8,128)S(1)}, f32[528,128]{1,0:T(8,128)S(1)}, u32[]{:S(2)}, u32[]{:S(2)}) collective-permute-start(f32[528,128]{1,0:T(8,128)S(1)} %get-tuple-element.39), channel_id=1, source_target_pairs={{0,1},{1,2},{2,3},{3,0},{4,5},{5,6},{6,7},{7,4},{8,9},{9,10},{10,1... | collective-permute-start | bytes 811016 | tf_op jit(solution)/shard_map/ppermute | solution.py:576
  41.7 7.4 %copy-start.4 = (f32[3,16,16,128]{3,2,1,0:T(8,128)S(1)}, f32[3,16,16,128]{3,2,1,0:T(8,128)}, u32[]{:S(2)}) copy-start(f32[3,16,16,128]{3,2,1,0:T(8,128)} %get-tuple-element.34.base) | copy-start | bytes 1179652
  41.7 7.4 %collective-permute-start.5 = (f32[528,128]{1,0:T(8,128)S(1)}, f32[528,128]{1,0:T(8,128)S(1)}, u32[]{:S(2)}, u32[]{:S(2)}) collective-permute-start(f32[528,128]{1,0:T(8,128)S(1)} %get-tuple-element.40), channel_id=1, source_target_pairs={{0,3},{1,0},{2,1},{3,2},{4,7},{5,4},{6,5},{7,6},{8,11},{9,8},{10,9... | collective-permute-start | bytes 811016 | tf_op jit(solution)/shard_map/ppermute | solution.py:576
  62.2 9.6 %collective-permute-start.6 = (f32[8,16,128]{2,1,0:T(8,128)S(1)}, f32[8,16,128]{2,1,0:T(8,128)S(1)}, u32[]{:S(2)}, u32[]{:S(2)}) collective-permute-start(f32[8,16,128]{2,1,0:T(8,128)S(1)} %get-tuple-element.47.sent_upper), channel_id=1, source_target_pairs={{0,4},{4,8},{8,12},{12,16},{16,20},{20,24},{24,28},{28,32},{32,36}... | collective-permute-start | bytes 196616 | tf_op jit(solution)/shard_map/ppermute | solution.py:576
  62.3 9.5 %collective-permute-start.7 = (f32[8,16,128]{2,1,0:T(8,128)S(1)}, f32[8,16,128]{2,1,0:T(8,128)S(1)}, u32[]{:S(2)}, u32[]{:S(2)}) collective-permute-start(f32[8,16,128]{2,1,0:T(8,128)S(1)} %get-tuple-element.46.sent_lower), channel_id=1, source_target_pairs={{0,252},{4,0},{8,4},{12,8},{16,12},{20,16},{24,20},{28,24},{32,28}... | collective-permute-start | bytes 196616 | tf_op jit(solution)/shard_map/ppermute | solution.py:576
  71.8 3.4 %collective-permute-start.8 = (f32[256,128]{1,0:T(8,128)S(1)}, f32[256,128]{1,0:T(8,128)S(1)}, u32[]{:S(2)}, u32[]{:S(2)}) collective-permute-start(f32[256,128]{1,0:T(8,128)S(1)} %get-tuple-element.51.sent_right), channel_id=1, source_target_pairs={{0,1},{1,2},{2,3},{3,0},{4,5},{5,6},{6,7},{7,4},{8,9},{9,10},{10,1... | collective-permute-start | bytes 393224 | tf_op jit(solution)/shard_map/ppermute | solution.py:576
  73.3 4.4 %collective-permute-start.9 = (f32[256,128]{1,0:T(8,128)S(1)}, f32[256,128]{1,0:T(8,128)S(1)}, u32[]{:S(2)}, u32[]{:S(2)}) collective-permute-start(f32[256,128]{1,0:T(8,128)S(1)} %get-tuple-element.50.sent_left), channel_id=1, source_target_pairs={{0,3},{1,0},{2,1},{3,2},{4,7},{5,4},{6,5},{7,6},{8,11},{9,8},{10,9... | collective-permute-start | bytes 393224 | tf_op jit(solution)/shard_map/ppermute | solution.py:576

commit v4 on v3

--- a/solution.py
+++ b/solution.py
@@ -365,10 +365,11 @@
 
 def rate_kernel(
     flow, latest, base, void, lower, upper, left, right, deposit,
-    history_out, trial_out, div_out, to_upper, to_lower, edge_out, scaled, rates, leaving,
+    history_out, trial_out, div_out, to_upper, to_lower, edge_out, scaled, rates, held, leaving,
 ):
-    copies = [pltpu.make_async_copy(latest, history_out.at[1], leaving.at[0])]
-    copies[0].start()
+    arrival = pltpu.make_async_copy(latest, held, leaving.at[5])
+    arrival.start()
+    copies = [pltpu.make_async_copy(held, history_out.at[1], leaving.at[0])]
     def void_layer(layer):
         if layer < 0:
             return lower[HALO + layer, :, :]
@@ -434,6 +435,9 @@
                 )
             )
             copies[-1].start()
+        if layer == 7:
+            arrival.wait()
+            copies[0].start()
     for layer in range(EDGE):
         total = div_out[layer, :, :]
         if layer < EDGE - 1:
@@ -632,7 +636,7 @@
         [(2, 3) + cells, (3,) + cells, cells, (REACH + 2,) + cells[1:], (REACH + 2,) + cells[1:], (2, EDGE, LANES)],
         (flow, latest, base, void, state_low, state_high, state_left, state_right, deposit),
         spaces={1: pltpu.HBM},
-        scratch=(pltpu.VMEM(cells, F32), pltpu.VMEM((3,) + cells, F32), pltpu.SemaphoreType.DMA((5,))),
+        scratch=(pltpu.VMEM(cells, F32), pltpu.VMEM((3,) + cells, F32), pltpu.VMEM((3,) + cells, F32), pltpu.SemaphoreType.DMA((6,))),
         far=(0,),
     )
     div_low = shifted(up, "gz", 1)

time: 80.1 us -> 69 us (0.86)
  Pallas kernels: 29.9 us -> 18.9 us
    pallas_call x10, Pallas kernels: 29.9 us -> 18.9 us  [call(): pl.pallas_call(kernel, out_shape=shapes, in_specs=[pl.BlockSpec(memory_sp...]
  transfers between devices with their start and end apart: 11 -> 11, of which waited for: 5 -> 5; matrix products, arithmetic and copies ran while one was open for 0% -> 0% of each run, Pallas kernels for 16% -> 18%
where the time goes in v4:
time: 69 us; the launch traced here: 68.8 us
  starting transfers between devices  37.1 us (54%)
  Pallas kernels  18.9 us (27%)
  waiting for transfers between devices  12 us (17%)
  between operations  0.81 us (1%)
    ppermute x10, starting transfers between devices, shifted(): lax.ppermute(value, axis, [(source, (source + steps) % count) for source...  30.2 us
    pallas_call x10, Pallas kernels, call(): pl.pallas_call(kernel, out_shape=shapes, in_specs=[pl.BlockSpec(memory_sp...  18.9 us
    ppermute x10, waiting for transfers between devices, shifted(): lax.ppermute(value, axis, [(source, (source + steps) % count) for source...  12 us
    all_to_all x1, starting transfers between devices, per_device(): lax.all_to_all(outgoing, 'gz', split_axis=0, concat_axis=0, tiled=True)  6.9 us
  transfers between devices with their start and end apart: 11, of which 5 were waited for; matrix products, arithmetic and copies ran while one was open for 0% of the time, Pallas kernels for 18%

profile of v4, /device:TPU:1, one launch (start us, length us, event | category | flops | bytes accessed | tf_op | source)
XLA Modules:
  0.0 68.8 jit_solution(6021937445333038297)
XLA Ops:
  0.6 0.0 copy-start.5
  0.6 0.0 copy-start.6
  0.7 0.0 copy-start.7
  0.7 0.0 copy-start.1
  0.7 2.2 %shard_map.103 = (f32[352,128]{1,0:T(8,128)S(1)}, f32[352,128]{1,0:T(8,128)S(1)}, s32[8,128]{1,0:T(8,128)S(1)}) custom-call(s32[32,64]{1,0:T(8,128)} %bitcast.7, f32[3,16,16,128]{3,2,1,0:T(8,128)} %velocity.3, f32[2,3,16,16,128]{4,3,2,1,0:T(8,128)} %history.3, f32[16,16,128]{2,1,0:T(8,128)} %pressure.3, f32[16,16,128]{2,1,0:T(8,128)} %void.3), custom_call_target="tpu_custom_call" | custom-call | tf_op jit(solution)/shard_map/pallas_call | solution.py:44
  2.9 0.0 copy-start
  2.9 3.8 %collective-permute-start = (f32[352,128]{1,0:T(8,128)S(1)}, f32[352,128]{1,0:T(8,128)S(1)}, u32[]{:S(2)}, u32[]{:S(2)}) collective-permute-start(f32[352,128]{1,0:T(8,128)S(1)} %get-tuple-element.30), channel_id=1, source_target_pairs={{0,4},{4,8},{8,12},{12,16},{16,20},{20,24},{24,28},{28,32},{32,36}... | collective-permute-start | bytes 540680 | tf_op jit(solution)/shard_map/ppermute | solution.py:580
  6.7 7.6 %collective-permute-start.1 = (f32[352,128]{1,0:T(8,128)S(1)}, f32[352,128]{1,0:T(8,128)S(1)}, u32[]{:S(2)}, u32[]{:S(2)}) collective-permute-start(f32[352,128]{1,0:T(8,128)S(1)} %get-tuple-element.31), channel_id=1, source_target_pairs={{0,252},{4,0},{8,4},{12,8},{16,12},{20,16},{24,20},{28,24},{32,28}... | collective-permute-start | bytes 540680 | tf_op jit(solution)/shard_map/ppermute | solution.py:580
  14.3 0.0 copy-done.5
  14.3 0.0 copy-done.6
  14.3 0.0 copy-done.7
  14.3 2.6 %shard_map.107 = f32[64,8,128]{2,1,0:T(8,128)} custom-call(f32[16,4096]{1,0:T(8,128)S(1)} %copy-done.5, s32[32,128]{1,0:T(8,128)S(1)} %bitcast.5, s32[32,128]{1,0:T(8,128)S(1)} %bitcast.6), custom_call_target="tpu_custom_call" | custom-call | tf_op jit(solution)/shard_map/pallas_call | solution.py:44
  16.9 0.0 copy-start.2
  16.9 0.0 copy-start.3
  16.9 6.9 %all-to-all-start = ((f32[64,8,128]{2,1,0:T(8,128)}), f32[64,8,128]{2,1,0:T(8,128)S(1)}, u32[]{:S(2)}, u32[]{:S(2)}) async-start(f32[64,8,128]{2,1,0:T(8,128)} %shard_map.107), calls=%async_computation | async-start | bytes 524288 | tf_op jit(solution)/shard_map/all_to_all | solution.py:607
  23.9 0.0 collective-permute-done.lower
  23.9 0.0 collective-permute-done.1.upper
  23.9 0.0 copy-done.1
  23.9 0.0 copy-done
  23.9 0.0 copy-done.2
  23.9 0.0 copy-done.3
  23.9 0.6 shard_map.105
  24.5 2.6 %collective-permute-start.2 = (f32[17,16,128]{2,1,0:T(8,128)S(1)}, f32[17,16,128]{2,1,0:T(8,128)S(1)}, u32[]{:S(2)}, u32[]{:S(2)}) collective-permute-start(f32[17,16,128]{2,1,0:T(8,128)S(1)} %get-tuple-element.36), channel_id=1, source_target_pairs={{0,4},{4,8},{8,12},{12,16},{16,20},{20,24},{24,28},{28,32},{32,36}... | collective-permute-start | bytes 417800 | tf_op jit(solution)/shard_map/ppermute | solution.py:580
  27.1 4.7 %collective-permute-start.3 = (f32[17,16,128]{2,1,0:T(8,128)S(1)}, f32[17,16,128]{2,1,0:T(8,128)S(1)}, u32[]{:S(2)}, u32[]{:S(2)}) collective-permute-start(f32[17,16,128]{2,1,0:T(8,128)S(1)} %get-tuple-element.37), channel_id=1, source_target_pairs={{0,252},{4,0},{8,4},{12,8},{16,12},{20,16},{24,20},{28,24},{32,28}... | collective-permute-start | bytes 417800 | tf_op jit(solution)/shard_map/ppermute | solution.py:580
  31.8 2.6 %shard_map.104 = (f32[3,16,16,128]{3,2,1,0:T(8,128)S(1)}, f32[3,16,16,128]{3,2,1,0:T(8,128)}, f32[3,16,16,128]{3,2,1,0:T(8,128)}) custom-call(s32[8,128]{1,0:T(8,128)S(1)} %get-tuple-element.29.codes, f32[3,16,16,128]{3,2,1,0:T(8,128)S(1)} %copy-done.1, f32[2,3,16,16,128]{4,3,2,1,0:T(8,128)S(1)} %copy-done, f32[16,16,128]{2,1,0:T(8,128)S(1)} %copy-done.2, ...), custom_call_target="tpu_custom_call" | custom-call | tf_op jit(solution)/shard_map/pallas_call | solution.py:44
  34.3 4.5 %collective-permute-done.2.lower = f32[17,16,128]{2,1,0:T(8,128)S(1)} collective-permute-done((f32[17,16,128]{2,1,0:T(8,128)S(1)}, f32[17,16,128]{2,1,0:T(8,128)S(1)}, u32[]{:S(2)}, u32[]{:S(2)}) %collective-permute-start.2) | collective-permute-done | bytes 139296 | tf_op jit(solution)/shard_map/ppermute | solution.py:580
  38.9 0.0 collective-permute-done.3.upper
  38.9 0.1 shard_map.106
  38.9 2.8 %collective-permute-start.4 = (f32[528,128]{1,0:T(8,128)S(1)}, f32[528,128]{1,0:T(8,128)S(1)}, u32[]{:S(2)}, u32[]{:S(2)}) collective-permute-start(f32[528,128]{1,0:T(8,128)S(1)} %get-tuple-element.39), channel_id=1, source_target_pairs={{0,1},{1,2},{2,3},{3,0},{4,5},{5,6},{6,7},{7,4},{8,9},{9,10},{10,1... | collective-permute-start | bytes 811016 | tf_op jit(solution)/shard_map/ppermute | solution.py:580
  41.7 0.0 copy-start.4
  41.7 0.0 collective-permute-start.5
  41.7 0.0 all-to-all-done.arrived
  41.7 6.3 %shard_map.108.deposit = f32[4,16,16,128]{3,2,1,0:T(8,128)S(1)} custom-call(f32[64,8,128]{2,1,0:T(8,128)S(1)} %all-to-all-done.arrived), custom_call_target="tpu_custom_call" | custom-call | tf_op jit(solution)/shard_map/pallas_call | solution.py:44
  48.0 0.0 collective-permute-done.4.left
  48.0 1.1 %collective-permute-done.5.right = f32[528,128]{1,0:T(8,128)S(1)} collective-permute-done((f32[528,128]{1,0:T(8,128)S(1)}, f32[528,128]{1,0:T(8,128)S(1)}, u32[]{:S(2)}, u32[]{:S(2)}) %collective-permute-start.5) | collective-permute-done | bytes 270368 | tf_op jit(solution)/shard_map/ppermute | solution.py:580
  49.2 0.0 copy-done.4
  49.2 2.0 %shard_map.109 = (f32[2,3,16,16,128]{4,3,2,1,0:T(8,128)}, f32[3,16,16,128]{3,2,1,0:T(8,128)S(1)}, f32[16,16,128]{2,1,0:T(8,128)S(1)}, f32[8,16,128]{2,1,0:T(8,12...) custom-call(f32[3,16,16,128]{3,2,1,0:T(8,128)S(1)} %get-tuple-element.32.flow, ...), custom_call_target="tpu_custom_call" | custom-call | tf_op jit(solution)/shard_map/pallas_call | solution.py:44
  51.2 0.1 collective-permute-start.6
  51.3 7.2 %collective-permute-start.7 = (f32[8,16,128]{2,1,0:T(8,128)S(1)}, f32[8,16,128]{2,1,0:T(8,128)S(1)}, u32[]{:S(2)}, u32[]{:S(2)}) collective-permute-start(f32[8,16,128]{2,1,0:T(8,128)S(1)} %get-tuple-element.46.sent_lower), channel_id=1, source_target_pairs={{0,252},{4,0},{8,4},{12,8},{16,12},{20,16},{24,20},{28,24},{32,28}... | collective-permute-start | bytes 196616 | tf_op jit(solution)/shard_map/ppermute | solution.py:580
  58.4 2.3 %collective-permute-done.6.lower = f32[8,16,128]{2,1,0:T(8,128)S(1)} collective-permute-done((f32[8,16,128]{2,1,0:T(8,128)S(1)}, f32[8,16,128]{2,1,0:T(8,128)S(1)}, u32[]{:S(2)}, u32[]{:S(2)}) %collective-permute-start.6) | collective-permute-done | bytes 65568 | tf_op jit(solution)/shard_map/ppermute | solution.py:580
  60.7 0.0 collective-permute-done.7.upper
  60.8 1.5 %collective-permute-start.8 = (f32[256,128]{1,0:T(8,128)S(1)}, f32[256,128]{1,0:T(8,128)S(1)}, u32[]{:S(2)}, u32[]{:S(2)}) collective-permute-start(f32[256,128]{1,0:T(8,128)S(1)} %get-tuple-element.51.sent_right), channel_id=1, source_target_pairs={{0,1},{1,2},{2,3},{3,0},{4,5},{5,6},{6,7},{7,4},{8,9},{9,10},{10,1... | collective-permute-start | bytes 393224 | tf_op jit(solution)/shard_map/ppermute | solution.py:580
  62.2 0.0 collective-permute-start.9
  62.3 0.4 shard_map.110
  62.7 1.5 %collective-permute-done.8.left = f32[256,128]{1,0:T(8,128)S(1)} collective-permute-done((f32[256,128]{1,0:T(8,128)S(1)}, f32[256,128]{1,0:T(8,128)S(1)}, u32[]{:S(2)}, u32[]{:S(2)}) %collective-permute-start.8) | collective-permute-done | bytes 131104 | tf_op jit(solution)/shard_map/ppermute | solution.py:580
  64.2 2.5 %collective-permute-done.9.right = f32[256,128]{1,0:T(8,128)S(1)} collective-permute-done((f32[256,128]{1,0:T(8,128)S(1)}, f32[256,128]{1,0:T(8,128)S(1)}, u32[]{:S(2)}, u32[]{:S(2)}) %collective-permute-start.9) | collective-permute-done | bytes 131104 | tf_op jit(solution)/shard_map/ppermute | solution.py:580
  66.7 2.1 %shard_map.112 = (f32[3,16,16,128]{3,2,1,0:T(8,128)}, f32[16,16,128]{2,1,0:T(8,128)}) custom-call(f32[3,16,16,128]{3,2,1,0:T(8,128)S(1)} %get-tuple-element.41.trial, f32[30,32,128]{2,1,0:T(8,128)S(1)} %get-tuple-element.42.void_wide, f32[30,32,128]{2,1,0:T(8,128)S(1)} %get-tuple-element.43.press_wide, f32[30,32,128]{2,1,0:T(8,128)S(1)} %get-tuple-element.44.factor, ...), custom_call_target="tpu_custom_call" | custom-call | tf_op jit(solution)/shard_map/pallas_call | solution.py:44
  (1 shorter events, 0.0 us)
Async XLA Ops:
  0.6 13.7 %copy-start.5 = (f32[16,4096]{1,0:T(8,128)S(1)}, f32[16,4096]{1,0:T(8,128)}, u32[]{:S(2)}) copy-start(f32[16,4096]{1,0:T(8,128)} %records.1) | copy-start | bytes 786436
  0.6 13.7 %copy-start.6 = (s32[4096,1]{0,1:T(1,128)S(1)}, s32[4096,1]{0,1:T(1,128)}, u32[]{:S(2)}) copy-start(s32[4096,1]{0,1:T(1,128)} %param.14) | copy-start | bytes 49156
  0.7 13.6 %copy-start.7 = (s32[4096]{0:T(1024)S(1)}, s32[4096]{0:T(1024)}, u32[]{:S(2)}) copy-start(s32[4096]{0:T(1024)} %param.15) | copy-start | bytes 49156
  0.7 23.2 %copy-start.1 = (f32[3,16,16,128]{3,2,1,0:T(8,128)S(1)}, f32[3,16,16,128]{3,2,1,0:T(8,128)}, u32[]{:S(2)}) copy-start(f32[3,16,16,128]{3,2,1,0:T(8,128)} %velocity.3) | copy-start | bytes 1179652
  2.9 21.0 %copy-start = (f32[2,3,16,16,128]{4,3,2,1,0:T(8,128)S(1)}, f32[2,3,16,16,128]{4,3,2,1,0:T(8,128)}, u32[]{:S(2)}) copy-start(f32[2,3,16,16,128]{4,3,2,1,0:T(8,128)} %history.3) | copy-start | bytes 2359300
  2.9 21.0 %collective-permute-start = (f32[352,128]{1,0:T(8,128)S(1)}, f32[352,128]{1,0:T(8,128)S(1)}, u32[]{:S(2)}, u32[]{:S(2)}) collective-permute-start(f32[352,128]{1,0:T(8,128)S(1)} %get-tuple-element.30), channel_id=1, source_target_pairs={{0,4},{4,8},{8,12},{12,16},{16,20},{20,24},{24,28},{28,32},{32,36}... | collective-permute-start | bytes 540680 | tf_op jit(solution)/shard_map/ppermute | solution.py:580
  6.7 17.2 %collective-permute-start.1 = (f32[352,128]{1,0:T(8,128)S(1)}, f32[352,128]{1,0:T(8,128)S(1)}, u32[]{:S(2)}, u32[]{:S(2)}) collective-permute-start(f32[352,128]{1,0:T(8,128)S(1)} %get-tuple-element.31), channel_id=1, source_target_pairs={{0,252},{4,0},{8,4},{12,8},{16,12},{20,16},{24,20},{28,24},{32,28}... | collective-permute-start | bytes 540680 | tf_op jit(solution)/shard_map/ppermute | solution.py:580
  16.9 7.0 %copy-start.2 = (f32[16,16,128]{2,1,0:T(8,128)S(1)}, f32[16,16,128]{2,1,0:T(8,128)}, u32[]{:S(2)}) copy-start(f32[16,16,128]{2,1,0:T(8,128)} %pressure.3) | copy-start | bytes 393220
  16.9 7.0 %copy-start.3 = (f32[16,16,128]{2,1,0:T(8,128)S(1)}, f32[16,16,128]{2,1,0:T(8,128)}, u32[]{:S(2)}) copy-start(f32[16,16,128]{2,1,0:T(8,128)} %void.3) | copy-start | bytes 393220
  16.9 24.8 %all-to-all-start = ((f32[64,8,128]{2,1,0:T(8,128)}), f32[64,8,128]{2,1,0:T(8,128)S(1)}, u32[]{:S(2)}, u32[]{:S(2)}) async-start(f32[64,8,128]{2,1,0:T(8,128)} %shard_map.107), calls=%async_computation | async-start | bytes 524288 | tf_op jit(solution)/shard_map/all_to_all | solution.py:607
  24.5 14.3 %collective-permute-start.2 = (f32[17,16,128]{2,1,0:T(8,128)S(1)}, f32[17,16,128]{2,1,0:T(8,128)S(1)}, u32[]{:S(2)}, u32[]{:S(2)}) collective-permute-start(f32[17,16,128]{2,1,0:T(8,128)S(1)} %get-tuple-element.36), channel_id=1, source_target_pairs={{0,4},{4,8},{8,12},{12,16},{16,20},{20,24},{24,28},{28,32},{32,36}... | collective-permute-start | bytes 417800 | tf_op jit(solution)/shard_map/ppermute | solution.py:580
  27.1 11.8 %collective-permute-start.3 = (f32[17,16,128]{2,1,0:T(8,128)S(1)}, f32[17,16,128]{2,1,0:T(8,128)S(1)}, u32[]{:S(2)}, u32[]{:S(2)}) collective-permute-start(f32[17,16,128]{2,1,0:T(8,128)S(1)} %get-tuple-element.37), channel_id=1, source_target_pairs={{0,252},{4,0},{8,4},{12,8},{16,12},{20,16},{24,20},{28,24},{32,28}... | collective-permute-start | bytes 417800 | tf_op jit(solution)/shard_map/ppermute | solution.py:580
  38.9 9.1 %collective-permute-start.4 = (f32[528,128]{1,0:T(8,128)S(1)}, f32[528,128]{1,0:T(8,128)S(1)}, u32[]{:S(2)}, u32[]{:S(2)}) collective-permute-start(f32[528,128]{1,0:T(8,128)S(1)} %get-tuple-element.39), channel_id=1, source_target_pairs={{0,1},{1,2},{2,3},{3,0},{4,5},{5,6},{6,7},{7,4},{8,9},{9,10},{10,1... | collective-permute-start | bytes 811016 | tf_op jit(solution)/shard_map/ppermute | solution.py:580
  41.7 7.4 %copy-start.4 = (f32[3,16,16,128]{3,2,1,0:T(8,128)S(1)}, f32[3,16,16,128]{3,2,1,0:T(8,128)}, u32[]{:S(2)}) copy-start(f32[3,16,16,128]{3,2,1,0:T(8,128)} %get-tuple-element.34.base) | copy-start | bytes 1179652
  41.7 7.4 %collective-permute-start.5 = (f32[528,128]{1,0:T(8,128)S(1)}, f32[528,128]{1,0:T(8,128)S(1)}, u32[]{:S(2)}, u32[]{:S(2)}) collective-permute-start(f32[528,128]{1,0:T(8,128)S(1)} %get-tuple-element.40), channel_id=1, source_target_pairs={{0,3},{1,0},{2,1},{3,2},{4,7},{5,4},{6,5},{7,6},{8,11},{9,8},{10,9... | collective-permute-start | bytes 811016 | tf_op jit(solution)/shard_map/ppermute | solution.py:580
  51.2 9.6 %collective-permute-start.6 = (f32[8,16,128]{2,1,0:T(8,128)S(1)}, f32[8,16,128]{2,1,0:T(8,128)S(1)}, u32[]{:S(2)}, u32[]{:S(2)}) collective-permute-start(f32[8,16,128]{2,1,0:T(8,128)S(1)} %get-tuple-element.47.sent_upper), channel_id=1, source_target_pairs={{0,4},{4,8},{8,12},{12,16},{16,20},{20,24},{24,28},{28,32},{32,36}... | collective-permute-start | bytes 196616 | tf_op jit(solution)/shard_map/ppermute | solution.py:580
  51.3 9.5 %collective-permute-start.7 = (f32[8,16,128]{2,1,0:T(8,128)S(1)}, f32[8,16,128]{2,1,0:T(8,128)S(1)}, u32[]{:S(2)}, u32[]{:S(2)}) collective-permute-start(f32[8,16,128]{2,1,0:T(8,128)S(1)} %get-tuple-element.46.sent_lower), channel_id=1, source_target_pairs={{0,252},{4,0},{8,4},{12,8},{16,12},{20,16},{24,20},{28,24},{32,28}... | collective-permute-start | bytes 196616 | tf_op jit(solution)/shard_map/ppermute | solution.py:580
  60.8 3.4 %collective-permute-start.8 = (f32[256,128]{1,0:T(8,128)S(1)}, f32[256,128]{1,0:T(8,128)S(1)}, u32[]{:S(2)}, u32[]{:S(2)}) collective-permute-start(f32[256,128]{1,0:T(8,128)S(1)} %get-tuple-element.51.sent_right), channel_id=1, source_target_pairs={{0,1},{1,2},{2,3},{3,0},{4,5},{5,6},{6,7},{7,4},{8,9},{9,10},{10,1... | collective-permute-start | bytes 393224 | tf_op jit(solution)/shard_map/ppermute | solution.py:580
  62.2 4.4 %collective-permute-start.9 = (f32[256,128]{1,0:T(8,128)S(1)}, f32[256,128]{1,0:T(8,128)S(1)}, u32[]{:S(2)}, u32[]{:S(2)}) collective-permute-start(f32[256,128]{1,0:T(8,128)S(1)} %get-tuple-element.50.sent_left), channel_id=1, source_target_pairs={{0,3},{1,0},{2,1},{3,2},{4,7},{5,4},{6,5},{7,6},{8,11},{9,8},{10,9... | collective-permute-start | bytes 393224 | tf_op jit(solution)/shard_map/ppermute | solution.py:580
